TPU v7x, 128 devices: a whole 4x4x4 slice. The times are simulated.
128 devices in a mesh: gx: 16 (over z_lo, x, core), gz: 8 (over y, z_hi).
Axes of the slice: x: 4, y: 4, z: 4 (z_hi: 2, z_lo: 2; z = z_hi * 2 + z_lo), core: 2. Of those that a mesh axis runs over, the one named last changes fastest.
Arguments:
- elevation: float32 [2048, 2048], P(('gx', 'gz')), may hold values from -2 to 2
- potential: float32 [2048, 2048], P(('gx', 'gz')), may hold values from -6 to 6
- tracer: float32 [2048, 64, 256], P('gx', 'gz'), may hold values from -6 to 6
- wind_speed: float32 [2048, 64, 256], P('gx', 'gz'), may hold values from -4 to 4
Outputs:
- new_elevation: float32 [2048, 2048], P(('gx', 'gz'))
- new_tracer: float32 [2048, 64, 256], P('gx', 'gz')
All inputs are finite; a program needn't handle non-finite values.
Results may differ from a plain program's by a relative error of at most 0.00019.
Values sent between devices are 32-bit elements; how exact they have to be, the bound alone decides.
No kernel may reach another device: no remote copies, remote signals or barrier semaphores. Data moves between devices by JAX's collectives and lax.ppermute only.
A program may use at most 128 MiB of HBM per device.

v0:
```python
import jax
import jax.numpy as jnp
from jax import lax
from jax.sharding import PartitionSpec as P

NS = 2048


TWO_PI = 6.283185307179586
DT_WAVE = 0.05
COLUMN_DEPTH = 32.0
DT_AIR = 0.1
NU_AIR = 0.2
PRECISE = lax.Precision.HIGHEST


def padded_2(shard, sides, width, wrap):
    for axis, dim in sides:
        size, length = (lax.axis_size(axis), shard.shape[dim])
        up = [(i, (i + 1) % size) for i in range(size if wrap else size - 1)]
        down = [(j, i) for i, j in up]
        last = lax.slice_in_dim(shard, length - width, length, axis=dim)
        leading = lax.slice_in_dim(shard, 0, width, axis=dim)
        before = lax.ppermute(last, axis, up)
        after = lax.ppermute(leading, axis, down)
        shard = jnp.concatenate([before, shard, after], axis=dim)
    return shard


def angle_table(row_count, col_count, length):
    row_index = jnp.arange(row_count, dtype=jnp.int32)
    col_index = jnp.arange(col_count, dtype=jnp.int32)
    product = row_index[:, None] * col_index[None, :] % length
    angles = product.astype(jnp.float32) * (TWO_PI / length)
    return (jnp.cos(angles), jnp.sin(angles))


def contract(pattern, real_part, imaginary, cosine, sine, sign_value, keep_imaginary):
    real_cosine = jnp.einsum(pattern, real_part, cosine, precision=PRECISE)
    real_sine = jnp.einsum(pattern, real_part, sine, precision=PRECISE)
    if imaginary is None:
        return (real_cosine, sign_value * real_sine)
    imag_sine = jnp.einsum(pattern, imaginary, sine, precision=PRECISE)
    out_real = real_cosine - sign_value * imag_sine
    if not keep_imaginary:
        return (out_real, None)
    imag_cosine = jnp.einsum(pattern, imaginary, cosine, precision=PRECISE)
    return (out_real, imag_cosine + sign_value * real_sine)


def twist_phase(real_part, imaginary, cosine, sine, sign_value):
    out_real = real_part * cosine - sign_value * imaginary * sine
    out_imag = imaginary * cosine + sign_value * real_part * sine
    return (out_real, out_imag)


def transform_last(real_part, imaginary, inverse, keep_imaginary):
    length = real_part.shape[-1]
    inner_size = 128
    outer_size = length // inner_size
    leading = real_part.shape[:-1]
    sign_value = 1.0 if inverse else -1.0
    cosine_outer, sine_outer = angle_table(outer_size, outer_size, outer_size)
    cosine_inner, sine_inner = angle_table(inner_size, inner_size, inner_size)
    cosine_twist, sine_twist = angle_table(outer_size, inner_size, length)
    real_part = real_part.reshape(leading + (outer_size, inner_size))
    if imaginary is not None:
        imaginary = imaginary.reshape(leading + (outer_size, inner_size))
    if not inverse:
        real_part, imaginary = contract(
            "...an,ak->...kn", real_part, imaginary, cosine_outer, sine_outer, sign_value, True
        )
        real_part, imaginary = twist_phase(
            real_part, imaginary, cosine_twist, sine_twist, sign_value
        )
        real_part, imaginary = contract(
            "...kn,nb->...kb", real_part, imaginary, cosine_inner, sine_inner, sign_value, True
        )
        return (real_part.reshape(leading + (length,)), imaginary.reshape(leading + (length,)))
    real_part, imaginary = contract(
        "...kb,bn->...kn", real_part, imaginary, cosine_inner, sine_inner, sign_value, True
    )
    real_part, imaginary = twist_phase(real_part, imaginary, cosine_twist, sine_twist, sign_value)
    real_part, imaginary = contract(
        "...kn,ka->...an",
        real_part,
        imaginary,
        cosine_outer,
        sine_outer,
        sign_value,
        keep_imaginary,
    )
    factor = 1.0 / length
    real_part = real_part.reshape(leading + (length,)) * factor
    if imaginary is None:
        return (real_part, None)
    return (real_part, imaginary.reshape(leading + (length,)) * factor)


def permuted_waves(positions, length):
    inner_size = 128
    outer_size = length // inner_size
    wave_index = positions // inner_size + outer_size * (positions % inner_size)
    signed = jnp.where(wave_index < length // 2, wave_index, wave_index - length).astype(
        jnp.float32
    ) * (TWO_PI / length)
    odd_wave = jnp.where(wave_index == length // 2, 0.0, signed)
    return (signed, odd_wave)


def block_start(block_rows):
    return (lax.axis_index("gx") * lax.axis_size("gz") + lax.axis_index("gz")) * block_rows


def to_columns(stacked):
    return lax.all_to_all(stacked, ("gx", "gz"), split_axis=3, concat_axis=2, tiled=True)


def to_rows(stacked):
    return lax.all_to_all(stacked, ("gx", "gz"), split_axis=2, concat_axis=3, tiled=True)


def spectra(fields):
    real_part, imaginary = transform_last(fields, None, False, True)
    stacked = jnp.stack([real_part, imaginary], 1)
    turned = jnp.swapaxes(to_columns(stacked), 2, 3)
    return transform_last(turned[:, 0], turned[:, 1], False, True)


def fields_back(real_part, imaginary):
    real_part, imaginary = transform_last(real_part, imaginary, True, True)
    stacked = jnp.swapaxes(jnp.stack([real_part, imaginary], 1), 2, 3)
    turned = to_rows(stacked)
    return transform_last(turned[:, 0], turned[:, 1], True, False)


def fields_from(spectrum_list):
    members = len(spectrum_list)
    real_part, unused = fields_back(
        jnp.stack([member[0] for member in spectrum_list]),
        jnp.stack([member[1] for member in spectrum_list]),
    )
    return [real_part[offset] for offset in range(members)]


def scaled(real_part, imaginary, factor):
    return (factor * real_part, factor * imaginary)


def derived(real_part, imaginary, factor):
    return (-factor * imaginary, factor * real_part)


def level_rims(field):
    padded = padded_2(field, (("gz", 1),), 1, False)
    bottom = lax.axis_index("gz") == 0
    top_device = lax.axis_index("gz") == lax.axis_size("gz") - 1
    lower_level = jnp.concatenate(
        [jnp.where(bottom, field[:, :1], padded[:, :1]), field[:, :-1]], 1
    )
    upper_level = jnp.concatenate(
        [field[:, 1:], jnp.where(top_device, field[:, -1:], padded[:, -1:])], 1
    )
    return (lower_level, upper_level)


def shards(elevation, potential, tracer, wind_speed):
    block_rows = elevation.shape[0]
    real_part, imaginary = spectra(jnp.stack([elevation, potential]))
    positions = block_start(block_rows) + jnp.arange(block_rows, dtype=jnp.int32)
    wave_y, odd_y = permuted_waves(positions, NS)
    wave_x, odd_x = permuted_waves(jnp.arange(NS, dtype=jnp.int32), NS)
    magnitude = jnp.sqrt(wave_x[None, :] * wave_x[None, :] + wave_y[:, None] * wave_y[:, None])
    squared = magnitude * magnitude
    magnitude_cube = squared * magnitude
    along_x = odd_x[None, :] + jnp.zeros_like(magnitude)
    along_y = odd_y[:, None] + jnp.zeros_like(magnitude)
    eta_real, eta_imag = (real_part[0], imaginary[0])
    phi_real, phi_imag = (real_part[1], imaginary[1])
    first_once, first_twice, first_thrice, slope_x, slope_y, speed_x, speed_y = fields_from(
        [
            scaled(phi_real, phi_imag, magnitude),
            scaled(phi_real, phi_imag, squared),
            scaled(phi_real, phi_imag, magnitude_cube),
            derived(eta_real, eta_imag, along_x),
            derived(eta_real, eta_imag, along_y),
            derived(phi_real, phi_imag, along_x),
            derived(phi_real, phi_imag, along_y),
        ]
    )
    second_field = -elevation * first_once
    real_part, imaginary = spectra(second_field[None])
    second_once, second_twice = fields_from(
        [scaled(real_part[0], imaginary[0], magnitude), scaled(real_part[0], imaginary[0], squared)]
    )
    third_field = -elevation * second_once - 0.5 * elevation * elevation * first_twice
    real_part, imaginary = spectra(third_field[None])
    third_list = fields_from([scaled(real_part[0], imaginary[0], magnitude)])
    third_once = third_list[0]
    vertical = (
        first_once
        + elevation * first_twice
        + 0.5 * elevation * elevation * first_thrice
        + second_once
        + elevation * second_twice
        + third_once
    )
    tendency = (
        -(slope_x * speed_x + slope_y * speed_y)
        + (1.0 + slope_x * slope_x + slope_y * slope_y) * vertical
    )
    new_elevation = elevation + DT_WAVE * tendency
    columns = tracer.shape[2]
    padded = padded_2(tracer, (("gx", 0),), 1, True)
    eastern = padded[2:]
    western = padded[:-2]
    northern = jnp.concatenate([tracer[:, :, 1:], tracer[:, :, -1:]], 2)
    southern = jnp.concatenate([tracer[:, :, :1], tracer[:, :, :-1]], 2)
    moved_tracer = tracer + DT_AIR * (
        -wind_speed * (eastern - western) * 0.5
        + NU_AIR * (eastern + western + northern + southern - 4.0 * tracer)
    )
    real_part, imaginary = spectra(new_elevation[None])
    slope_list = fields_from([derived(real_part[0], imaginary[0], along_x)])
    new_slope = slope_list[0]
    window = jnp.stack([elevation[:, :columns], new_elevation[:, :columns], new_slope[:, :columns]])
    surface = lax.all_gather(window, "gz", axis=1, tiled=True)
    old_rows = surface[0]
    new_rows = surface[1]
    slope_rows = surface[2]
    levels = tracer.shape[1]
    level_count = levels * lax.axis_size("gz")
    sigma_level = (
        (lax.axis_index("gz") * levels + jnp.arange(levels, dtype=jnp.int32)).astype(jnp.float32)
        + 0.5
    ) / level_count
    lift_factor = (1.0 - sigma_level)[None, :, None]
    level_shift = (
        ((new_rows - old_rows) / (COLUMN_DEPTH - old_rows))[:, None, :] * lift_factor * level_count
    )
    lower_level, upper_level = level_rims(moved_tracer)
    remapped = (
        moved_tracer
        + 0.5 * level_shift * (upper_level - lower_level)
        + 0.5 * level_shift * level_shift * (upper_level - 2.0 * moved_tracer + lower_level)
    )
    lower_level, upper_level = level_rims(remapped)
    column_depth = (COLUMN_DEPTH - new_rows)[:, None, :]
    advection = (
        wind_speed
        * lift_factor
        * slope_rows[:, None, :]
        / column_depth
        * (upper_level - lower_level)
        * (0.5 * level_count)
    )
    spread_term = (
        NU_AIR
        * (upper_level - 2.0 * remapped + lower_level)
        * (level_count * level_count)
        / (column_depth * column_depth)
    )
    new_tracer = remapped + DT_AIR * (advection + spread_term)
    return (new_elevation, new_tracer)


def solution(mesh):
    return jax.shard_map(
        shards,
        mesh=mesh,
        in_specs=(
            P(("gx", "gz"), None),
            P(("gx", "gz"), None),
            P("gx", "gz", None),
            P("gx", "gz", None),
        ),
        out_specs=(P(("gx", "gz"), None), P("gx", "gz", None)),
        check_vma=False,
    )
```

profile of v0, /device:TPU:8, one launch (start us, length us, event | category | flops | bytes accessed | tf_op | source)
XLA Modules:
  0.0 606.4 jit_solution(7506074649540263558)
XLA Ops:
  10.3 7.0 %fusion.923 = f32[2048,2,2,16]{3,2,1,0:T(2,128)} fusion(f32[2,1,16,2048]{2,1,0,3:T(1,128)} %bitcast.800, f32[2,1,16,2048]{2,1,0,3:T(1,128)S(1)} %bitcast.798), kind=kLoop, calls=%fused_computation.1021 | loop fusion | flops 131072 | bytes 1048576
  17.3 8.0 %reshape.1070 = f32[128,1,1024]{2,1,0:T(1,128)} reshape(f32[2048,2,2,16]{3,2,1,0:T(2,128)} %fusion.923) | data formatting | bytes 1048576
  25.3 10.8 %all-to-all-start = ((f32[128,1,1024]{2,1,0:T(1,128)}), f32[128,1,1024]{2,1,0:T(1,128)S(1)}, u32[]{:S(2)}, u32[]{:S(2)}) async-start(f32[128,1,1024]{2,1,0:T(1,128)} %reshape.1070), calls=%async_computation | async-start | bytes 1048576 | tf_op jit(solution)/shard_map/all_to_all | solution.py:116
  36.1 12.8 %all-to-all-done = f32[128,1,1024]{2,1,0:T(1,128)S(1)} async-done(((f32[128,1,1024]{2,1,0:T(1,128)}), f32[128,1,1024]{2,1,0:T(1,128)S(1)}, u32[]{:S(2)}, u32[]{:S(2)}) %all-to-all-start) | async-done | bytes 524320 | tf_op jit(solution)/shard_map/all_to_all | solution.py:116
  51.5 6.9 %reshape.1071 = f32[2048,2,2,16]{3,2,1,0:T(2,128)} reshape(f32[128,1024]{1,0:T(8,128)S(1)} %reduce) | data formatting | bytes 1048576
  58.5 6.6 %copy.542 = f32[2,2,16,128,16]{2,3,4,1,0:T(8,128)} copy(f32[2,2,16,128,16]{2,1,0,4,3:T(2,128)} %bitcast.781) | data formatting | bytes 1048576 | tf_op jit(solution)/shard_map/all_to_all | solution.py:116
  65.1 4.9 all_to_all.107
  84.8 16.8 %copy.276 = f32[7,1,16,2048]{2,1,0,3:T(1,128)} copy(f32[7,1,16,2048]{3,2,0,1:T(8,128)} %mul.3195) | data formatting | bytes 1835008 | tf_op jit(solution)/shard_map/mul | solution.py:94
  103.9 12.4 %copy.277 = f32[7,1,16,2048]{2,1,0,3:T(1,128)} copy(f32[7,1,16,2048]{3,2,0,1:T(8,128)S(1)} %mul.3198) | data formatting | bytes 1835008 | tf_op jit(solution)/shard_map/mul | solution.py:97
  116.3 19.0 %fusion.921 = f32[2048,7,2,16]{3,2,1,0:T(2,128)} fusion(f32[7,1,16,2048]{2,1,0,3:T(1,128)} %copy.277, f32[7,1,16,2048]{2,1,0,3:T(1,128)} %copy.276), kind=kLoop, calls=%fused_computation.1019 | loop fusion | flops 458752 | bytes 3670016
  135.4 22.7 %reshape.1072 = f32[128,1,3584]{2,1,0:T(1,128)} reshape(f32[2048,7,2,16]{3,2,1,0:T(2,128)} %fusion.921) | data formatting | bytes 3670016
  158.1 31.8 %all_to_all.144 = f32[128,1,3584]{2,1,0:T(1,128)S(1)} all-to-all(f32[128,1,3584]{2,1,0:T(1,128)} %reshape.1072), channel_id=1, replica_groups=mesh['gx'=16,'gz'=8] {'gx','gz'}, dimensions={0} | all-to-all | bytes 3670016 | tf_op jit(solution)/shard_map/all_to_all | solution.py:120
  189.9 6.7 %reduce.1 = f32[128,3584]{1,0:T(8,128)} reduce(f32[128,1,3584]{2,1,0:T(1,128)S(1)} %all_to_all.144, f32[]{:T(128)} %broadcast.1810), dimensions={1}, to_apply=%all_to_all.108.reduce_sub_computation | reduce | bytes 3670020 | tf_op jit(solution)/shard_map/all_to_all | solution.py:120
  196.6 22.7 %reshape.1073 = f32[2048,7,2,16]{3,2,1,0:T(2,128)} reshape(f32[128,3584]{1,0:T(8,128)} %reduce.1) | data formatting | bytes 3670016
  219.3 18.8 %copy.540 = f32[7,2,128,16,16]{4,2,3,1,0:T(8,128)} copy(f32[7,2,128,16,16]{4,1,0,3,2:T(2,128)} %bitcast.779) | data formatting | bytes 3670016 | tf_op jit(solution)/shard_map/all_to_all | solution.py:120
  238.1 13.0 %all_to_all.111 = f32[7,2,16,2048]{3,2,1,0:T(8,128)S(1)} reshape(f32[7,2,16,128,16]{4,3,2,1,0:T(8,128)} %bitcast.780) | data formatting | bytes 3670016 | tf_op jit(solution)/shard_map/all_to_all | solution.py:120
  266.5 5.2 all-to-all-start.2
  283.4 4.1 reshape.1075
  287.5 4.1 copy.547
  306.3 7.4 %fusion.922 = f32[2048,2,2,16]{3,2,1,0:T(2,128)} fusion(f32[2,1,16,2048]{2,1,0,3:T(1,128)} %bitcast.801, f32[2,1,16,2048]{2,1,0,3:T(1,128)} %bitcast.799), kind=kLoop, calls=%fused_computation.1020 | loop fusion | flops 131072 | bytes 1048576
  313.7 8.0 %reshape.1076 = f32[128,1,1024]{2,1,0:T(1,128)} reshape(f32[2048,2,2,16]{3,2,1,0:T(2,128)} %fusion.922) | data formatting | bytes 1048576
  321.6 6.1 %all-to-all-start.3 = ((f32[128,1,1024]{2,1,0:T(1,128)}), f32[128,1,1024]{2,1,0:T(1,128)S(1)}, u32[]{:S(2)}, u32[]{:S(2)}) async-start(f32[128,1,1024]{2,1,0:T(1,128)} %reshape.1076), calls=%async_computation.3 | async-start | bytes 1048576 | tf_op jit(solution)/shard_map/all_to_all | solution.py:120
  330.0 10.7 %all-to-all-done.3 = f32[128,1,1024]{2,1,0:T(1,128)S(1)} async-done(((f32[128,1,1024]{2,1,0:T(1,128)}), f32[128,1,1024]{2,1,0:T(1,128)S(1)}, u32[]{:S(2)}, u32[]{:S(2)}) %all-to-all-start.3) | async-done | bytes 524320 | tf_op jit(solution)/shard_map/all_to_all | solution.py:120
  342.7 6.9 %reshape.1077 = f32[2048,2,2,16]{3,2,1,0:T(2,128)} reshape(f32[128,1024]{1,0:T(8,128)S(1)} %reduce.3) | data formatting | bytes 1048576
  349.6 6.6 %copy.541 = f32[2,2,128,16,16]{4,2,3,1,0:T(8,128)} copy(f32[2,2,128,16,16]{4,1,0,3,2:T(2,128)} %bitcast.783) | data formatting | bytes 1048576 | tf_op jit(solution)/shard_map/all_to_all | solution.py:120
  356.2 5.2 all_to_all.119
  370.9 5.0 reshape.1078
  375.9 5.0 all-to-all-start.4
  382.1 9.2 %all-to-all-done.4 = f32[128,1,512]{2,1,0:T(1,128)S(1)} async-done(((f32[128,1,512]{2,1,0:T(1,128)}), f32[128,1,512]{2,1,0:T(1,128)S(1)}, u32[]{:S(2)}, u32[]{:S(2)}) %all-to-all-start.4) | async-done | bytes 262176 | tf_op jit(solution)/shard_map/all_to_all | solution.py:116
  392.6 4.1 reshape.1079
  396.8 4.1 copy.546
  415.9 5.4 reshape.1080
  421.3 5.8 all-to-all-start.5
  430.7 5.3 collective-permute-start.2
  440.3 4.1 reshape.1081
  444.5 4.1 copy.545
  460.5 5.0 reshape.1082
  465.5 11.2 %all-to-all-start.6 = ((f32[128,1,512]{2,1,0:T(1,128)}), f32[128,1,512]{2,1,0:T(1,128)}, u32[]{:S(2)}, u32[]{:S(2)}) async-start(f32[128,1,512]{2,1,0:T(1,128)} %reshape.1082), calls=%async_computation.6 | async-start | bytes 524288 | tf_op jit(solution)/shard_map/all_to_all | solution.py:116
  477.8 9.0 %all-to-all-done.6 = f32[128,1,512]{2,1,0:T(1,128)} async-done(((f32[128,1,512]{2,1,0:T(1,128)}), f32[128,1,512]{2,1,0:T(1,128)}, u32[]{:S(2)}, u32[]{:S(2)}) %all-to-all-start.6) | async-done | bytes 262176 | tf_op jit(solution)/shard_map/all_to_all | solution.py:116
  489.7 5.1 reshape.1083
  494.8 4.1 copy.544
  518.7 5.2 reshape.1084
  523.9 5.8 all-to-all-start.7
  532.7 7.1 %all-to-all-done.7 = f32[128,1,512]{2,1,0:T(1,128)} async-done(((f32[128,1,512]{2,1,0:T(1,128)}), f32[128,1,512]{2,1,0:T(1,128)}, u32[]{:S(2)}, u32[]{:S(2)}) %all-to-all-start.7) | async-done | bytes 262176 | tf_op jit(solution)/shard_map/all_to_all | solution.py:120
  542.1 4.1 reshape.1085
  546.3 4.1 copy.543
  556.5 33.7 %all_gather.3 = f32[3,128,256]{2,1,0:T(8,128)S(1)} all-gather(f32[3,16,256]{2,1,0:T(8,128)S(1)} %pad_maximum_fusion.14), channel_id=1, replica_groups=mesh['gx'=16,'gz'=8] {'gz'}, dimensions={1}, use_global_device_ids=true | all-gather | bytes 442368 | tf_op jit(solution)/shard_map/all_gather | solution.py:227
  599.4 4.2 collective-permute-done.5
  (284 shorter events, 167.1 us)
Async XLA Ops:
  25.3 23.7 %all-to-all-start = ((f32[128,1,1024]{2,1,0:T(1,128)}), f32[128,1,1024]{2,1,0:T(1,128)S(1)}, u32[]{:S(2)}, u32[]{:S(2)}) async-start(f32[128,1,1024]{2,1,0:T(1,128)} %reshape.1070), calls=%async_computation | async-start | bytes 1048576 | tf_op jit(solution)/shard_map/all_to_all | solution.py:116
  257.0 1.8 copy-start.2
  258.8 106.8 %copy-start.3 = (f32[1,16,16,128]{3,2,1,0:T(8,128)}, f32[1,16,16,128]{3,2,1,0:T(8,128)S(1)}, u32[]{:S(2)}) copy-start(f32[1,16,16,128]{3,2,1,0:T(8,128)S(1)} %get-tuple-element.32) | copy-start | bytes 393220
  266.5 15.6 %all-to-all-start.2 = ((f32[128,1,512]{2,1,0:T(1,128)}), f32[128,1,512]{2,1,0:T(1,128)S(1)}, u32[]{:S(2)}, u32[]{:S(2)}) async-start(f32[128,1,512]{2,1,0:T(1,128)} %reshape.1074), calls=%async_computation.2 | async-start | bytes 524288 | tf_op jit(solution)/shard_map/all_to_all | solution.py:116
  272.4 154.8 %collective-permute-start = (f32[1,8,256]{2,0,1:T(1,128)S(1)}, f32[1,8,256]{2,0,1:T(1,128)S(1)}, u32[]{:S(2)}, u32[]{:S(2)}) collective-permute-start(f32[1,8,256]{2,0,1:T(1,128)S(1)} %copy.322), channel_id=1, source_target_pairs={{8,0},{16,8},{24,16},{32,24},{40,32},{48,40},{56,48},{64,56},{72,6... | collective-permute-start | bytes 24584 | tf_op jit(solution)/shard_map/ppermute | solution.py:25
  276.0 151.2 %collective-permute-start.1 = (f32[1,8,256]{2,0,1:T(1,128)S(1)}, f32[1,8,256]{2,0,1:T(1,128)S(1)}, u32[]{:S(2)}, u32[]{:S(2)}) collective-permute-start(f32[1,8,256]{2,0,1:T(1,128)S(1)} %copy.324), channel_id=1, source_target_pairs={{0,8},{8,16},{16,24},{24,32},{32,40},{40,48},{48,56},{56,64},{64,7... | collective-permute-start | bytes 24584 | tf_op jit(solution)/shard_map/ppermute | solution.py:24
  321.6 19.1 %all-to-all-start.3 = ((f32[128,1,1024]{2,1,0:T(1,128)}), f32[128,1,1024]{2,1,0:T(1,128)S(1)}, u32[]{:S(2)}, u32[]{:S(2)}) async-start(f32[128,1,1024]{2,1,0:T(1,128)} %reshape.1076), calls=%async_computation.3 | async-start | bytes 1048576 | tf_op jit(solution)/shard_map/all_to_all | solution.py:120
  365.5 3.1 copy-start.5
  375.9 15.4 %all-to-all-start.4 = ((f32[128,1,512]{2,1,0:T(1,128)}), f32[128,1,512]{2,1,0:T(1,128)S(1)}, u32[]{:S(2)}, u32[]{:S(2)}) async-start(f32[128,1,512]{2,1,0:T(1,128)} %reshape.1078), calls=%async_computation.4 | async-start | bytes 524288 | tf_op jit(solution)/shard_map/all_to_all | solution.py:116
  415.9 11.2 %copy-start = (f32[128,8,256]{2,1,0:T(8,128)S(1)}, f32[128,8,256]{2,1,0:T(8,128)}, u32[]{:S(2)}) copy-start(f32[128,8,256]{2,1,0:T(8,128)} %param.7) | copy-start | bytes 3145732
  421.3 16.7 %all-to-all-start.5 = ((f32[128,1,512]{2,1,0:T(1,128)}), f32[128,1,512]{2,1,0:T(1,128)}, u32[]{:S(2)}, u32[]{:S(2)}) async-start(f32[128,1,512]{2,1,0:T(1,128)} %reshape.1080), calls=%async_computation.5 | async-start | bytes 524288 | tf_op jit(solution)/shard_map/all_to_all | solution.py:120
  430.7 99.0 %collective-permute-start.2 = (f32[128,1,256]{2,0,1:T(8,128)}, f32[128,1,256]{2,0,1:T(8,128)}, u32[]{:S(2)}, u32[]{:S(2)}) collective-permute-start(f32[128,1,256]{2,0,1:T(8,128)} %get-tuple-element.20), channel_id=1, source_target_pairs={{1,0},{2,1},{3,2},{4,3},{5,4},{6,5},{7,6},{9,8},{10,9},{11,10},{12... | collective-permute-start | bytes 393224 | tf_op jit(solution)/shard_map/ppermute | solution.py:25
  436.0 93.7 %collective-permute-start.3 = (f32[128,1,256]{2,0,1:T(8,128)}, f32[128,1,256]{2,0,1:T(8,128)}, u32[]{:S(2)}, u32[]{:S(2)}) collective-permute-start(f32[128,1,256]{2,0,1:T(8,128)} %get-tuple-element.21), channel_id=1, source_target_pairs={{0,1},{1,2},{2,3},{3,4},{4,5},{5,6},{6,7},{8,9},{9,10},{10,11},{11... | collective-permute-start | bytes 393224 | tf_op jit(solution)/shard_map/ppermute | solution.py:24
  451.7 2.9 copy-start.4
  451.7 2.9 copy-start.6
  451.7 2.9 copy-start.8
  451.7 2.9 copy-start.9
  451.8 2.9 copy-start.10
  451.8 2.9 copy-start.11
  455.0 0.7 copy-start.7
  465.5 21.3 %all-to-all-start.6 = ((f32[128,1,512]{2,1,0:T(1,128)}), f32[128,1,512]{2,1,0:T(1,128)}, u32[]{:S(2)}, u32[]{:S(2)}) async-start(f32[128,1,512]{2,1,0:T(1,128)} %reshape.1082), calls=%async_computation.6 | async-start | bytes 524288 | tf_op jit(solution)/shard_map/all_to_all | solution.py:116
  523.9 16.0 %all-to-all-start.7 = ((f32[128,1,512]{2,1,0:T(1,128)}), f32[128,1,512]{2,1,0:T(1,128)}, u32[]{:S(2)}, u32[]{:S(2)}) async-start(f32[128,1,512]{2,1,0:T(1,128)} %reshape.1084), calls=%async_computation.7 | async-start | bytes 524288 | tf_op jit(solution)/shard_map/all_to_all | solution.py:120
  553.6 2.9 copy-start.13
  553.6 2.9 copy-start.14
  553.6 36.6 %copy-start.1 = (f32[128,7,256]{2,0,1:T(8,128)S(1)}, f32[128,7,256]{2,0,1:T(8,128)}, u32[]{:S(2)}) copy-start(f32[128,7,256]{2,0,1:T(8,128)} %get-tuple-element.17) | copy-start | bytes 2752516
  553.6 36.6 %copy-start.12 = (f32[128,1,256]{2,0,1:T(8,128)S(1)}, f32[128,1,256]{2,0,1:T(8,128)}, u32[]{:S(2)}) copy-start(f32[128,1,256]{2,0,1:T(8,128)} %get-tuple-element.19) | copy-start | bytes 393220
  553.6 36.6 %copy-start.15 = (f32[8]{0:T(128)S(1)}, f32[8]{0:T(128)}, u32[]{:S(2)}) copy-start(f32[8]{0:T(128)} %multiply_subtract_fusion.18) | copy-start | bytes 100
  591.0 8.4 %collective-permute-start.4 = (f32[128,1,256]{2,0,1:T(8,128)S(1)}, f32[128,1,256]{2,0,1:T(8,128)S(1)}, u32[]{:S(2)}, u32[]{:S(2)}) collective-permute-start(f32[128,1,256]{2,0,1:T(8,128)S(1)} %get-tuple-element.14), channel_id=1, source_target_pairs={{1,0},{2,1},{3,2},{4,3},{5,4},{6,5},{7,6},{9,8},{10,9},{11,10},{12... | collective-permute-start | bytes 393224 | tf_op jit(solution)/shard_map/ppermute | solution.py:25
  594.2 9.3 %collective-permute-start.5 = (f32[128,1,256]{2,0,1:T(8,128)S(1)}, f32[128,1,256]{2,0,1:T(8,128)S(1)}, u32[]{:S(2)}, u32[]{:S(2)}) collective-permute-start(f32[128,1,256]{2,0,1:T(8,128)S(1)} %get-tuple-element.15), channel_id=1, source_target_pairs={{0,1},{1,2},{2,3},{3,4},{4,5},{5,6},{6,7},{8,9},{9,10},{10,11},{11... | collective-permute-start | bytes 393224 | tf_op jit(solution)/shard_map/ppermute | solution.py:24
where the time goes:
time: 617 us; the launch traced here: 606 us
  local copies, waits for them, and re-layouts  285 us (46%)
  starting transfers between devices  68.5 us (11%)
  blocking collectives  65.5 us (11%)
  matrix products  63.7 us (10%)
  other arithmetic  63 us (10%)
  waiting for transfers between devices  57.8 us (9%)
    unnamed x80, local copies, waits for them, and re-layouts  133 us
    all_to_all x8, local copies, waits for them, and re-layouts, to_rows(): lax.all_to_all(stacked, ('gx', 'gz'), split_axis=2, concat_axis=3, tiled=...  58.2 us
    all_to_all x4, waiting for transfers between devices, to_columns(): lax.all_to_all(stacked, ('gx', 'gz'), split_axis=3, concat_axis=2, tiled=...  34.8 us
    all_to_all x9, local copies, waits for them, and re-layouts, to_columns(): lax.all_to_all(stacked, ('gx', 'gz'), split_axis=3, concat_axis=2, tiled=...  34.7 us
    unnamed x15, other arithmetic  34.3 us
    all_gather x1, blocking collectives, shards(): surface = lax.all_gather(window, 'gz', axis=1, tiled=True)  33.7 us
    all_to_all x4, starting transfers between devices, to_columns(): lax.all_to_all(stacked, ('gx', 'gz'), split_axis=3, concat_axis=2, tiled=...  32.1 us
    all_to_all x1, blocking collectives, to_rows(): lax.all_to_all(stacked, ('gx', 'gz'), split_axis=2, concat_axis=3, tiled=...  31.8 us
  transfers between devices with their start and end apart: 13, of which 8 were waited for; matrix products, arithmetic and copies ran while one was open for 27% of the time, Pallas kernels for 0%

commit v1 on v0

v1 whole, which is shorter than its diff:
```python
import functools

import jax
import jax.numpy as jnp
import ml_dtypes
import numpy as np
from jax import lax
from jax.experimental import pallas as pl
from jax.experimental.pallas import tpu as pltpu
from jax.sharding import PartitionSpec as P

NS = 2048
DT_WAVE = 0.05
COLUMN_DEPTH = 32.0
DT_AIR = 0.1
NU_AIR = 0.2
TWO_PI = 6.283185307179586
WAVE_UNIT = TWO_PI / NS
BOTH = ("gx", "gz")
F32 = jnp.float32
BF16 = jnp.bfloat16


def halves(matrix):
    exact = np.asarray(matrix, np.float64)
    lead = exact.astype(np.float32).astype(ml_dtypes.bfloat16)
    rest = (exact - lead.astype(np.float64)).astype(np.float32).astype(ml_dtypes.bfloat16)
    return np.stack([lead, rest])


@functools.cache
def tables():
    n128, n16 = np.arange(128), np.arange(16)
    eye16, eye8 = np.eye(16), np.eye(8)
    turn = 2 * np.pi * (np.outer(n128, n128) % 128) / 128
    c, s = np.cos(turn), np.sin(turn)
    far = np.block([[c, s], [-s, c]])
    edge = np.zeros((2, 128, 2, 128))
    edge_back = np.zeros((2, 128, 2, 128))
    sign = (-1.0) ** n128
    for d in range(128):
        if d < 64:
            angle, part = 2 * np.pi * n128 * d / 128, 0
        else:
            angle, part = 2 * np.pi * n128 * (2 * (d - 64) + 1) / 256, 1
        edge[0, d, part] = np.cos(angle)
        edge[1, d, part] = -np.sin(angle) if d else sign
        weight = 2.0 if d else 1.0
        edge_back[part, :, 0, d] = weight * np.cos(angle)
        edge_back[part, :, 1, d] = -weight * np.sin(angle) if d else sign
    edge = edge.reshape(256, 256)
    edge_back = edge_back.reshape(256, 256)
    k8 = np.arange(8)
    angle = 2 * np.pi * np.outer(n16, k8) / 16
    near_re, near_im = np.cos(angle), -np.sin(angle)
    near_im[:, 0] = (-1.0) ** n16
    weight = np.where(k8 == 0, 1.0, 2.0)
    near = np.zeros((16, 16, 2, 8, 16))
    near_back = np.zeros((2, 8, 16, 16, 16))
    for part, table in enumerate((near_re, near_im)):
        near[:, :, part] = table[:, None, :, None] * eye16[None, :, None, :]
        near_back[part] = (table * weight).T[:, None, :, None] * eye16[None, :, None, :]
    near = near.reshape(256, 256)
    near_back = near_back.reshape(256, 256)
    angle = 2 * np.pi * np.outer(n16, n16) / 16
    cx, sx = np.kron(eye8, np.cos(angle)), np.kron(eye8, np.sin(angle))
    side = np.block([[cx, -sx], [sx, cx]])
    y_angle = 2 * np.pi * np.repeat(np.outer(n128, k8), 16, axis=1) / NS
    x_angle = 2 * np.pi * np.tile(np.outer(n128, n16), (1, 8)) / NS
    twist = lambda a: np.stack([np.cos(a), -np.sin(a)]).astype(np.float32)
    r = n128[None, :, None, None]
    x = 16 * n128[None, None, :, None] + n16.reshape(4, 1, 1, 4)
    n = r - x
    with np.errstate(divide="ignore", invalid="ignore"):
        slope = np.where(n % NS == 0, 0.0, (np.pi / NS) * (-1.0) ** (n % 2) / np.tan(np.pi * n / NS))
    slope = slope.reshape(512, 512)
    return dict(
        far=halves(far),
        far_back=halves(far.T),
        edge=halves(edge),
        edge_back=halves(edge_back),
        near=halves(near),
        near_back=halves(near_back),
        side=halves(side),
        side_back=halves(side.T),
        twist_y=twist(y_angle),
        twist_x=twist(x_angle),
        slope=halves(slope),
    )


def dot(a, b):
    return jnp.dot(a, b, preferred_element_type=F32)


def split(x):
    lead = x.astype(BF16)
    return lead, (x - lead.astype(F32)).astype(BF16)


def from_left(table, x):
    lead, rest = split(x)
    width = x.shape[1]
    both = dot(table[0], jnp.concatenate([lead, rest], 1))
    return both[:, :width] + both[:, width:] + dot(table[1], lead)


def from_right(x, table):
    lead, rest = split(x)
    rows = x.shape[0]
    both = dot(jnp.concatenate([lead, rest], 0), table[0])
    return both[:rows] + both[rows:] + dot(lead, table[1])


def slot_zero(shape):
    return lax.broadcasted_iota(jnp.int32, shape, 1) % 128 < 16


def y_forward(t, field):
    parts = from_right(field, t["near"])
    re, im = parts[:, :128], parts[:, 128:]
    c, s = t["twist_y"][0], t["twist_y"][1]
    parts = jnp.concatenate([re * c - im * s, re * s + im * c], 0)
    usual = from_left(t["far"], parts)
    first = from_left(t["edge"], parts)
    out = jnp.where(slot_zero(usual.shape), first, usual)
    return out[:128], out[128:]


def y_back(t, re, im):
    parts = jnp.concatenate([re, im], 0)
    usual = from_left(t["far_back"], parts)
    first = from_left(t["edge_back"], parts)
    parts = jnp.where(slot_zero(usual.shape), first, usual)
    re, im = parts[:128], parts[128:]
    c, s = t["twist_y"][0], t["twist_y"][1]
    parts = jnp.concatenate([re * c + im * s, im * c - re * s], 1)
    return from_right(parts, t["near_back"])


def x_forward(t, re, im, mirrored):
    parts = jnp.concatenate([re, im], 0)
    if mirrored:
        parts = jnp.concatenate([parts, jnp.concatenate([re, -im], 0)], 1)
    parts = from_left(t["far"], parts)
    c, s = t["twist_x"][0], t["twist_x"][1]
    rows = []
    for at in range(0, parts.shape[1], 128):
        re, im = parts[:128, at : at + 128], parts[128:, at : at + 128]
        rows.append(jnp.concatenate([re * c - im * s, re * s + im * c], 1))
    parts = from_right(jnp.concatenate(rows, 0) if mirrored else rows[0], t["side"])
    out = parts[:128, :128], parts[:128, 128:]
    if mirrored:
        out += parts[128:, :128], parts[128:, 128:]
    return out


def x_back(t, re, im):
    parts = from_right(jnp.concatenate([re, im], 1), t["side_back"])
    re, im = parts[:, :128], parts[:, 128:]
    c, s = t["twist_x"][0], t["twist_x"][1]
    parts = jnp.concatenate([re * c + im * s, im * c - re * s], 0)
    out = from_left(t["far_back"], parts)
    return out[:128], out[128:]


def x_waves():
    q1 = lax.broadcasted_iota(jnp.int32, (128, 128), 0)
    lane = lax.broadcasted_iota(jnp.int32, (128, 128), 1)
    kx = q1 + 128 * (lane % 16)
    return jnp.where(kx < NS // 2, kx, kx - NS)


def odd_x():
    kx = x_waves()
    return jnp.where(kx == -(NS // 2), 0, kx).astype(F32) * WAVE_UNIT


def squared_waves(device):
    slot = lax.broadcasted_iota(jnp.int32, (128, 128), 1) // 16
    first = jnp.where(device < 64, 16 * device, 8 + 16 * (device - 64))
    ky = jnp.where(slot == 0, first, slot + 16 * device)
    other = jnp.where((slot == 0) & (device == 0), NS // 2, ky)
    fold = lambda k: jnp.where(k > NS // 2, NS - k, k).astype(F32) * WAVE_UNIT
    wave_x = x_waves().astype(F32) * WAVE_UNIT
    return wave_x * wave_x + fold(ky) * fold(ky), wave_x * wave_x + fold(other) * fold(other)


def even_filter(spectrum, on_re, on_im):
    re, im, mirror_re, mirror_im = spectrum
    plus = (on_re + on_im) * (0.5 / (NS * NS))
    minus = (on_re - on_im) * (0.5 / (NS * NS))
    return re * plus + mirror_re * minus, im * plus + mirror_im * minus


def power_filter(spectrum, squares, power):
    factors = []
    for square in squares:
        magnitude = jnp.sqrt(square)
        factors.append({1: magnitude, 2: square, 3: square * magnitude}[power])
    return even_filter(spectrum, *factors)


def x_derivative(re, im, scale):
    factor = odd_x() * scale
    return -factor * im, factor * re


def y_derivative(re, im):
    d = lax.broadcasted_iota(jnp.int32, (128, 128), 0)
    slot = lax.broadcasted_iota(jnp.int32, (128, 128), 1) // 16
    first = jnp.where(d < 64, 16 * d, 8 + 16 * (d - 64))
    ky = jnp.where(slot == 0, first, slot + 16 * d)
    factor = jnp.where(ky < NS // 2, ky, ky - NS).astype(F32) * (WAVE_UNIT / NS)
    return -factor * im, factor * re


def to_lanes(rows):
    return jnp.concatenate([rows[:, 128 * a : 128 * a + 128] for a in range(16)], 0).T


def pick(ref, fields, index):
    step = 2 * fields
    return ref[pl.ds(2 * index, 128, step), :], ref[pl.ds(2 * index + 1, 128, step), :]


def put(ref, fields, index, values):
    step = 2 * fields
    ref[pl.ds(2 * index, 128, step), :] = values[0]
    ref[pl.ds(2 * index + 1, 128, step), :] = values[1]


def run(body, names, outs, *arrays, scalars=None, scratch=()):
    consts = [jnp.asarray(tables()[name]) for name in names]
    lead = [] if scalars is None else [scalars]

    def kernel(*refs):
        at = len(lead)
        held = dict(zip(names, refs[at : at + len(names)]))
        body(held, *refs[:at], *refs[at + len(names) :])

    vmem = pl.BlockSpec(memory_space=pltpu.VMEM)
    smem = pl.BlockSpec(memory_space=pltpu.SMEM)
    return pl.pallas_call(
        kernel,
        out_shape=[jax.ShapeDtypeStruct(shape, F32) for shape in outs],
        in_specs=[smem] * len(lead) + [vmem] * (len(consts) + len(arrays)),
        out_specs=[vmem] * len(outs),
        scratch_shapes=list(scratch),
        name=body.__name__,
    )(*lead, *consts, *arrays)


Y_FWD = ("near", "far", "edge", "twist_y")
Y_BACK = ("near_back", "far_back", "edge_back", "twist_y")
Y_BOTH = ("near", "far", "edge", "twist_y", "near_back", "far_back", "edge_back")
X_BOTH = ("far", "side", "twist_x", "far_back", "side_back")
X_BACK = ("twist_x", "far_back", "side_back")
PLANES = (256, 128)
FIELD = (128, 256)


def rows_start(t, phi, send, speed):
    spectrum = y_forward(t, to_lanes(phi[...]))
    put(send, 1, 0, spectrum)
    speed[...] = y_back(t, *y_derivative(*spectrum))


def rows_surface(t, eta, send, lanes, slope):
    lanes[...] = to_lanes(eta[...])
    spectrum = y_forward(t, lanes[...])
    put(send, 1, 0, spectrum)
    slope[...] = y_back(t, *y_derivative(*spectrum))


def columns_first(t, device, got, send, later):
    spectrum = x_forward(t, *pick(got, 1, 0), True)
    squares = squared_waves(device[0])
    put(send, 2, 0, x_back(t, *power_filter(spectrum, squares, 1)))
    put(send, 2, 1, x_back(t, *power_filter(spectrum, squares, 2)))
    put(later, 2, 0, power_filter(spectrum, squares, 3))
    put(later, 2, 1, x_derivative(spectrum[0], spectrum[1], 1.0 / (NS * NS)))


def columns_later(t, held, send):
    for index in range(2):
        put(send, 2, index, x_back(t, *pick(held, 2, index)))


def rows_second(t, got, lanes, surface, send, once, twice):
    once[...] = y_back(t, *pick(got, 2, 0))
    put(send, 2, 0, y_forward(t, -lanes[...] * once[...]))
    put(send, 2, 1, pick(surface, 1, 0))
    twice[...] = y_back(t, *pick(got, 2, 1))


def columns_second(t, device, got, later, send, slope):
    spectrum = x_forward(t, *pick(got, 2, 0), True)
    squares = squared_waves(device[0])
    put(send, 4, 0, x_back(t, *power_filter(spectrum, squares, 1)))
    put(send, 4, 1, x_back(t, *power_filter(spectrum, squares, 2)))
    put(send, 4, 2, pick(later, 2, 0))
    put(send, 4, 3, pick(later, 2, 1))
    re, im = x_forward(t, *pick(got, 2, 1), False)
    put(slope, 1, 0, x_back(t, *x_derivative(re, im, 1.0 / (NS * NS))))


def rows_third(t, got, lanes, once, twice, send, sums, speed):
    eta = lanes[...]
    second_once = y_back(t, *pick(got, 4, 0))
    third = -eta * second_once - 0.5 * eta * eta * twice[...]
    put(send, 1, 0, y_forward(t, third))
    second_twice = y_back(t, *pick(got, 4, 1))
    thrice = y_back(t, *pick(got, 4, 2))
    speed[...] = y_back(t, *pick(got, 4, 3))
    sums[...] = (
        once[...]
        + eta * twice[...]
        + 0.5 * eta * eta * thrice
        + second_once
        + eta * second_twice
    )


def columns_third(t, device, got, slope, send):
    spectrum = x_forward(t, *pick(got, 1, 0), True)
    put(send, 2, 0, x_back(t, *power_filter(spectrum, squared_waves(device[0]), 1)))
    put(send, 2, 1, pick(slope, 1, 0))


def rows_finish(t, got, lanes, sums, speed_x, speed_y, slope_y, new_rows, send, window):
    third_once = y_back(t, *pick(got, 2, 0))
    slope_x = y_back(t, *pick(got, 2, 1))
    eta, along = lanes[...], slope_y[...]
    tendency = -(slope_x * speed_x[...] + along * speed_y[...]) + (
        1.0 + slope_x * slope_x + along * along
    ) * (sums[...] + third_once)
    new = (eta + DT_WAVE * tendency).T
    for a in range(16):
        new_rows[:, 128 * a : 128 * a + 128] = new[16 * a : 16 * a + 16]
    window[0:32, :] = new[:32]
    window[32:64, :] = eta.T[:32]
    group = lax.broadcasted_iota(jnp.int32, (16, 128), 1) // 32
    blocks = []
    for a in range(2):
        rows = new[16 * a : 16 * a + 16]
        turned = [rows] + [pltpu.roll(rows, 32 * k, 1) for k in range(1, 4)]
        for chunk in range(4):
            block = jnp.zeros((4, 128), F32)
            for g in range(4):
                moved = turned[(g - chunk) % 4]
                block = block + jnp.where(group == g, moved, 0.0)[4 * g : 4 * g + 4]
            blocks.append(block)
    block = jnp.concatenate(blocks, 0)
    for at in range(16):
        send[32 * at : 32 * at + 32, :] = block


def columns_slope(t, slab, got, window, send, twofold):
    twofold[0:512, :] = got[...]
    twofold[512:1024, :] = got[...]
    start = pl.multiple_of(slab[0] * 32, 32)
    full = from_left(t["slope"], twofold[pl.ds(start, 512), :])
    group = lax.broadcasted_iota(jnp.int32, (128, 128), 1) // 32
    total = jnp.zeros((128, 128), F32)
    for g in range(4):
        total = total + jnp.where(group == g, full[128 * g : 128 * g + 128], 0.0)
    total = total + pltpu.roll(total, 64, 1)
    total = total + pltpu.roll(total, 32, 1)
    slope = total.T[:32]
    for at in range(8):
        send[96 * at : 96 * at + 32, :] = slope
        send[96 * at + 32 : 96 * at + 96, :] = window[...]


def air_finish(got, moved, wind, below, above, place, out, slope_s, new_s, old_s):
    step = pl.program_id(0)
    depth = out.shape[0]

    @pl.when(step == 0)
    def _():
        slope_t = jnp.concatenate([got[96 * g : 96 * g + 32, :] for g in range(8)], 0)
        slope_s[...] = slope_t.T
        for g in range(8):
            for a in range(2):
                at = 96 * g + 32 + 16 * a
                rows, lanes = slice(16 * g, 16 * g + 16), slice(128 * a, 128 * a + 128)
                new_s[rows, lanes] = got[at : at + 16, :]
                old_s[rows, lanes] = got[at + 32 : at + 48, :]

    here = pl.ds(pl.multiple_of(step * depth, depth), depth)
    slope, new, old = slope_s[here, :], new_s[here, :], old_s[here, :]
    group, levels = place[0], moved.shape[1]
    total = levels * place[1]
    ratio = (new - old) / (COLUMN_DEPTH - old) * total.astype(F32)
    inverse = 1.0 / (COLUMN_DEPTH - new)
    level = lax.broadcasted_iota(jnp.int32, (levels, 256), 0)
    lift = 1.0 - ((group * levels + level).astype(F32) + 0.5) / total.astype(F32)
    lift_below = 1.0 - ((group * levels - 1).astype(F32) + 0.5) / total.astype(F32)
    lift_above = 1.0 - ((group * levels + levels).astype(F32) + 0.5) / total.astype(F32)
    bottom, top = group == 0, group == place[1] - 1

    def remap(lower, mid, upper, shift):
        return (
            mid + 0.5 * shift * (upper - lower) + 0.5 * shift * shift * (upper - 2.0 * mid + lower)
        )

    advect = slope * inverse * (DT_AIR * 0.5 * total.astype(F32))
    spread = inverse * inverse * (DT_AIR * NU_AIR * (total * total).astype(F32))
    for x in range(depth):
        row = slice(x, x + 1)
        m = moved[x]
        outer_low, low = below[x, 0:1], below[x, 1:2]
        high, outer_high = above[x, 0:1], above[x, 1:2]
        low = jnp.where(bottom, m[:1], low)
        high = jnp.where(top, m[levels - 1 :], high)
        lower = jnp.where(level == 0, low, pltpu.roll(m, 1, 0))
        upper = jnp.where(level == levels - 1, high, pltpu.roll(m, levels - 1, 0))
        shift = ratio[row] * lift
        r = remap(lower, m, upper, shift)
        r_low = remap(outer_low, low, m[:1], ratio[row] * lift_below)
        r_high = remap(m[levels - 1 :], high, outer_high, ratio[row] * lift_above)
        r_low = jnp.where(bottom, r[:1], r_low)
        r_high = jnp.where(top, r[levels - 1 :], r_high)
        lower = jnp.where(level == 0, r_low, pltpu.roll(r, 1, 0))
        upper = jnp.where(level == levels - 1, r_high, pltpu.roll(r, levels - 1, 0))
        out[x] = (
            r
            + wind[x] * lift * advect[row] * (upper - lower)
            + spread[row] * (upper - 2.0 * r + lower)
        )


def air_call(got, moved, wind, below, above, place):
    depth = 16
    block = pl.BlockSpec((depth, 8, 256), lambda i: (i, 0, 0))
    rim = pl.BlockSpec((depth, 2, 256), lambda i: (i, 0, 0))
    return pl.pallas_call(
        air_finish,
        out_shape=jax.ShapeDtypeStruct(moved.shape, F32),
        grid=(moved.shape[0] // depth,),
        in_specs=[
            pl.BlockSpec(got.shape, lambda i: (0, 0)),
            block,
            block,
            rim,
            rim,
            pl.BlockSpec(memory_space=pltpu.SMEM),
        ],
        out_specs=block,
        scratch_shapes=[pltpu.VMEM((128, 256), F32)] * 3,
        name="air_finish",
    )(got, moved, wind, below, above, place)


def moved_air(tracer, wind_speed):
    size = lax.axis_size("gx")
    up = [(i, (i + 1) % size) for i in range(size)]
    down = [(j, i) for i, j in up]
    before = lax.ppermute(tracer[-1:], "gx", up)
    after = lax.ppermute(tracer[:1], "gx", down)
    western = jnp.concatenate([before, tracer[:-1]], 0)
    eastern = jnp.concatenate([tracer[1:], after], 0)
    northern = jnp.concatenate([tracer[:, :, 1:], tracer[:, :, -1:]], 2)
    southern = jnp.concatenate([tracer[:, :, :1], tracer[:, :, :-1]], 2)
    moved = tracer + DT_AIR * (
        -wind_speed * (eastern - western) * 0.5
        + NU_AIR * (eastern + western + northern + southern - 4.0 * tracer)
    )
    size = lax.axis_size("gz")
    up = [(i, i + 1) for i in range(size - 1)]
    down = [(j, i) for i, j in up]
    below = lax.ppermute(moved[:, -2:], "gz", up)
    above = lax.ppermute(moved[:, :2], "gz", down)
    return moved, below, above


def exchange(buffer, axes=BOTH):
    return lax.all_to_all(buffer, axes, split_axis=0, concat_axis=0, tiled=True)


def shards(elevation, potential, tracer, wind_speed):
    gx, gz = lax.axis_index("gx"), lax.axis_index("gz")
    device = (gx * lax.axis_size("gz") + gz).astype(jnp.int32).reshape(1)
    slab = gx.astype(jnp.int32).reshape(1)
    place = jnp.stack([gz, lax.axis_size("gz")]).astype(jnp.int32)

    send, speed_y = run(rows_start, Y_BOTH, [PLANES, FIELD], potential)
    got = exchange(send)
    surface, lanes, slope_y = run(rows_surface, Y_BOTH, [PLANES, FIELD, FIELD], elevation)
    moved, below, above = moved_air(tracer, wind_speed)

    send, later = run(columns_first, X_BOTH, [(512, 128), (512, 128)], got, scalars=device)
    got = exchange(send)
    (later,) = run(columns_later, X_BACK, [(512, 128)], later)

    send, once, twice = run(
        rows_second, Y_BOTH, [(512, 128), FIELD, FIELD], got, lanes, surface
    )
    got = exchange(send)
    send, slope = run(columns_second, X_BOTH, [(1024, 128), PLANES], got, later, scalars=device)
    got = exchange(send)
    send, sums, speed_x = run(
        rows_third, Y_BOTH, [PLANES, FIELD, FIELD], got, lanes, once, twice
    )
    got = exchange(send)
    (send,) = run(columns_third, X_BOTH, [(512, 128)], got, slope, scalars=device)
    got = exchange(send)
    new_rows, send, window = run(
        rows_finish,
        Y_BACK,
        [(16, NS), (512, 128), (64, 128)],
        got,
        lanes,
        sums,
        speed_x,
        speed_y,
        slope_y,
    )
    got = exchange(send)
    (send,) = run(
        columns_slope,
        ("slope",),
        [(768, 128)],
        got,
        window,
        scalars=slab,
        scratch=[pltpu.VMEM((1024, 128), F32)],
    )
    got = exchange(send, "gz")
    return new_rows, air_call(got, moved, wind_speed, below, above, place)


def solution(mesh):
    return jax.shard_map(
        shards,
        mesh=mesh,
        in_specs=(P(BOTH, None), P(BOTH, None), P("gx", "gz", None), P("gx", "gz", None)),
        out_specs=(P(BOTH, None), P("gx", "gz", None)),
        check_vma=False,
    )
```

time: 617 us -> 179 us (0.29); the launches traced: 606 us -> 178 us
  local copies, waits for them, and re-layouts: 285 us -> 10.3 us
  blocking collectives: 65.5 us -> 0 us
  matrix products: 63.7 us -> 0 us
  other arithmetic: 63 us -> 3.82 us
  Pallas kernels: 0 us -> 40.1 us
  starting transfers between devices: 68.5 us -> 54.9 us
  waiting for transfers between devices: 57.8 us -> 67.9 us
    unnamed x80 -> x26, local copies, waits for them, and re-layouts: 133 us -> 5.87 us
    all_to_all x17 -> x0, local copies, waits for them, and re-layouts: 92.9 us -> none  [the longest x8 58.2 us: to_rows(): lax.all_to_all(stacked, ('gx', 'gz'), split_axis=2, concat_axis=3, tiled=...]
    dot_general x112 -> x0, matrix products: 63.7 us -> none  [the longest x32 16.6 us: contract(): real_cosine = jnp.einsum(pattern, real_part, cosine, precision=PRECISE)]
    pallas_call x0 -> x11, Pallas kernels: none -> 40.1 us  [the longest x10 32.9 us: run(): pl.pallas_call(kernel, out_shape=[jax.ShapeDtypeStruct(shape, F32) for sh...]
    mul x10 -> x0, local copies, waits for them, and re-layouts: 36.1 us -> none  [the longest x5 20.8 us: transform_last(): real_part = real_part.reshape(leading + (length,)) * factor]
    unnamed x15 -> x0, other arithmetic: 34.3 us -> none
    all_gather x1 -> x0, blocking collectives: 33.7 us -> none  [shards(): surface = lax.all_gather(window, 'gz', axis=1, tiled=True)]
    all_to_all x1 -> x0, blocking collectives: 31.8 us -> none  [to_rows(): lax.all_to_all(stacked, ('gx', 'gz'), split_axis=2, concat_axis=3, tiled=...]
  transfers between devices with their start and end apart: 13 -> 12, of which waited for: 8 -> 8; matrix products, arithmetic and copies ran while one was open for 27% -> 5% of each run, Pallas kernels for 0% -> 9%
where the time goes in v1:
time: 179 us; the launch traced here: 178 us
  waiting for transfers between devices  67.9 us (38%)
  starting transfers between devices  54.9 us (31%)
  Pallas kernels  40.1 us (22%)
  local copies, waits for them, and re-layouts  10.3 us (6%)
  other arithmetic  3.82 us (2%)
    all_to_all x8, waiting for transfers between devices, exchange(): return lax.all_to_all(buffer, axes, split_axis=0, concat_axis=0, tiled=True)  57 us
    all_to_all x8, starting transfers between devices, exchange(): return lax.all_to_all(buffer, axes, split_axis=0, concat_axis=0, tiled=True)  43.9 us
    pallas_call x10, Pallas kernels, run(): pl.pallas_call(kernel, out_shape=[jax.ShapeDtypeStruct(shape, F32) for sh...  32.9 us
    ppermute x1, waiting for transfers between devices, moved_air(): above = lax.ppermute(moved[:, :2], 'gz', down)  10.9 us
    pallas_call x1, Pallas kernels, air_call(): pl.pallas_call(air_finish, out_shape=jax.ShapeDtypeStruct(moved.shape, F3...  7.19 us
    unnamed x26, local copies, waits for them, and re-layouts  5.87 us
    ppermute x1, starting transfers between devices, moved_air(): above = lax.ppermute(moved[:, :2], 'gz', down)  4.87 us
    ppermute x1, starting transfers between devices, moved_air(): after = lax.ppermute(tracer[:1], 'gx', down)  3.69 us
  transfers between devices with their start and end apart: 12, of which 8 were waited for; matrix products, arithmetic and copies ran while one was open for 5% of the time, Pallas kernels for 9%

profile of v1, /device:TPU:8, one launch (start us, length us, event | category | flops | bytes accessed | tf_op | source)
XLA Modules:
  0.0 177.9 jit_solution(17542291888469748478)
XLA Ops:
  0.6 3.2 %rows_start.1 = (f32[256,128]{1,0:T(8,128)}, f32[128,256]{1,0:T(8,128)}) custom-call(bf16[2,256,256]{2,1,0:T(8,128)(2,1)} %constant.43.clone.refs_0_, bf16[2,256,256]{2,1,0:T(8,128)(2,1)} %constant.44.clone.refs_1_, bf16[2,256,256]{2,1,0:T(8,128)(2,1)} %constant.45.clone.refs_2_, f32[2,128,128]{2,1,0:T(8,128)} %constant.46.clone.refs_3_, ...), custom_call_target="tpu_custom_call" | custom-call | tf_op jit(solution)/shard_map/rows_start/pallas_call | solution.py:244
  3.8 10.4 %all-to-all-start = ((f32[128,2,128]{2,1,0:T(2,128)}), f32[128,2,128]{2,1,0:T(2,128)S(1)}, u32[]{:S(2)}, u32[]{:S(2)}) async-start(f32[128,2,128]{2,1,0:T(2,128)} %bitcast.33), calls=%async_computation | async-start | bytes 262144 | tf_op jit(solution)/shard_map/all_to_all | solution.py:479
  14.3 9.2 %all-to-all-done = f32[128,2,128]{2,1,0:T(2,128)S(1)} async-done(((f32[128,2,128]{2,1,0:T(2,128)}), f32[128,2,128]{2,1,0:T(2,128)S(1)}, u32[]{:S(2)}, u32[]{:S(2)}) %all-to-all-start) | async-done | bytes 131104 | tf_op jit(solution)/shard_map/all_to_all | solution.py:479
  23.5 0.7 copy-done.9
  24.2 3.2 %columns_first.1 = (f32[512,128]{1,0:T(8,128)}, f32[512,128]{1,0:T(8,128)}) custom-call(s32[1]{0:T(128)} %bitcast.refs_0_, bf16[2,256,256]{2,1,0:T(8,128)(2,1)} %constant.44.clone.refs_1_, bf16[2,256,256]{2,1,0:T(8,128)(2,1)} %constant.50.clone.refs_2_, f32[2,128,128]{2,1,0:T(8,128)} %constant.51.clone.refs_3_.refs_0_, ...), custom_call_target="tpu_custom_call" | custom-call | tf_op jit(solution)/shard_map/columns_first/pallas_call | solution.py:244
  27.3 4.8 %all-to-all-start.1 = ((f32[128,4,128]{2,1,0:T(4,128)}), f32[128,4,128]{2,1,0:T(4,128)S(1)}, u32[]{:S(2)}, u32[]{:S(2)}) async-start(f32[128,4,128]{2,1,0:T(4,128)} %bitcast.32), calls=%async_computation.1 | async-start | bytes 524288 | tf_op jit(solution)/shard_map/all_to_all | solution.py:479
  32.1 3.2 %rows_surface.1 = (f32[256,128]{1,0:T(8,128)}, f32[128,256]{1,0:T(8,128)}, f32[128,256]{1,0:T(8,128)}) custom-call(bf16[2,256,256]{2,1,0:T(8,128)(2,1)} %constant.43.clone.refs_0_, bf16[2,256,256]{2,1,0:T(8,128)(2,1)} %constant.44.clone.refs_1_, bf16[2,256,256]{2,1,0:T(8,128)(2,1)} %constant.45.clone.refs_2_, f32[2,128,128]{2,1,0:T(8,128)} %constant.46.clone.refs_3_, ...), custom_call_target="tpu_custom_call" | custom-call | tf_op jit(solution)/shard_map/rows_surface/pallas_call | solution.py:244
  35.3 7.3 %all-to-all-done.1 = f32[128,4,128]{2,1,0:T(4,128)S(1)} async-done(((f32[128,4,128]{2,1,0:T(4,128)}), f32[128,4,128]{2,1,0:T(4,128)S(1)}, u32[]{:S(2)}, u32[]{:S(2)}) %all-to-all-start.1) | async-done | bytes 262176 | tf_op jit(solution)/shard_map/all_to_all | solution.py:479
  42.6 0.7 copy-done.7
  43.3 3.5 %rows_second.1 = (f32[512,128]{1,0:T(8,128)}, f32[128,256]{1,0:T(8,128)}, f32[128,256]{1,0:T(8,128)}) custom-call(bf16[2,256,256]{2,1,0:T(8,128)(2,1)} %constant.43.clone.refs_0_, bf16[2,256,256]{2,1,0:T(8,128)(2,1)} %constant.44.clone.refs_1_, bf16[2,256,256]{2,1,0:T(8,128)(2,1)} %constant.45.clone.refs_2_, f32[2,128,128]{2,1,0:T(8,128)} %constant.46.clone.refs_3_, ...), custom_call_target="tpu_custom_call" | custom-call | tf_op jit(solution)/shard_map/rows_second/pallas_call | solution.py:244
  46.9 4.8 %all-to-all-start.2 = ((f32[128,4,128]{2,1,0:T(4,128)}), f32[128,4,128]{2,1,0:T(4,128)S(1)}, u32[]{:S(2)}, u32[]{:S(2)}) async-start(f32[128,4,128]{2,1,0:T(4,128)} %bitcast.31), calls=%async_computation.2 | async-start | bytes 524288 | tf_op jit(solution)/shard_map/all_to_all | solution.py:479
  51.7 2.5 %columns_later.1.refs_7_ = f32[512,128]{1,0:T(8,128)} custom-call(f32[2,128,128]{2,1,0:T(8,128)} %constant.51.clone.refs_3_.refs_0_, bf16[2,256,256]{2,1,0:T(8,128)(2,1)} %constant.48.clone.refs_5_.refs_4_.refs_1_, bf16[2,256,256]{2,1,0:T(8,128)(2,1)} %constant.52.clone.refs_5_.refs_2_, f32[512,128]{1,0:T(8,128)} %get-tuple-element.25.refs_3_), custom_call_target="tpu_custom_call" | custom-call | tf_op jit(solution)/shard_map/columns_later/pallas_call | solution.py:244
  54.1 8.1 %all-to-all-done.2 = f32[128,4,128]{2,1,0:T(4,128)S(1)} async-done(((f32[128,4,128]{2,1,0:T(4,128)}), f32[128,4,128]{2,1,0:T(4,128)S(1)}, u32[]{:S(2)}, u32[]{:S(2)}) %all-to-all-start.2) | async-done | bytes 262176 | tf_op jit(solution)/shard_map/all_to_all | solution.py:479
  62.2 0.7 copy-done.8
  62.9 4.1 %columns_second.1 = (f32[1024,128]{1,0:T(8,128)}, f32[256,128]{1,0:T(8,128)}) custom-call(s32[1]{0:T(128)} %bitcast.refs_0_, bf16[2,256,256]{2,1,0:T(8,128)(2,1)} %constant.44.clone.refs_1_, bf16[2,256,256]{2,1,0:T(8,128)(2,1)} %constant.50.clone.refs_2_, f32[2,128,128]{2,1,0:T(8,128)} %constant.51.clone.refs_3_.refs_0_, ...), custom_call_target="tpu_custom_call" | custom-call | tf_op jit(solution)/shard_map/columns_second/pallas_call | solution.py:244
  67.0 4.8 %all-to-all-start.3 = ((f32[128,8,128]{2,1,0:T(8,128)}), f32[128,8,128]{2,1,0:T(8,128)S(1)}, u32[]{:S(2)}, u32[]{:S(2)}) async-start(f32[128,8,128]{2,1,0:T(8,128)} %bitcast.29), calls=%async_computation.3 | async-start | bytes 1048576 | tf_op jit(solution)/shard_map/all_to_all | solution.py:479
  71.8 3.7 %collective-permute-start = (f32[1,8,256]{2,1,0:T(8,128)S(1)}, f32[1,8,256]{2,1,0:T(8,128)S(1)}, u32[]{:S(2)}, u32[]{:S(2)}) collective-permute-start(f32[1,8,256]{2,1,0:T(8,128)S(1)} %get-tuple-element.42), channel_id=1, source_target_pairs={{8,0},{16,8},{24,16},{32,24},{40,32},{48,40},{56,48},{64,56},{72,6... | collective-permute-start | bytes 24584 | tf_op jit(solution)/shard_map/ppermute | solution.py:461
  75.5 0.0 collective-permute-start.1
  75.5 1.7 fusion.10
  77.2 7.9 %all-to-all-done.3 = f32[128,8,128]{2,1,0:T(8,128)S(1)} async-done(((f32[128,8,128]{2,1,0:T(8,128)}), f32[128,8,128]{2,1,0:T(8,128)S(1)}, u32[]{:S(2)}, u32[]{:S(2)}) %all-to-all-start.3) | async-done | bytes 524320 | tf_op jit(solution)/shard_map/all_to_all | solution.py:479
  85.0 0.8 copy-done.3
  85.8 4.3 %rows_third.1 = (f32[256,128]{1,0:T(8,128)}, f32[128,256]{1,0:T(8,128)}, f32[128,256]{1,0:T(8,128)}) custom-call(bf16[2,256,256]{2,1,0:T(8,128)(2,1)} %constant.43.clone.refs_0_, bf16[2,256,256]{2,1,0:T(8,128)(2,1)} %constant.44.clone.refs_1_, bf16[2,256,256]{2,1,0:T(8,128)(2,1)} %constant.45.clone.refs_2_, f32[2,128,128]{2,1,0:T(8,128)} %constant.46.clone.refs_3_, ...), custom_call_target="tpu_custom_call" | custom-call | tf_op jit(solution)/shard_map/rows_third/pallas_call | solution.py:244
  90.1 4.6 %all-to-all-start.4 = ((f32[128,2,128]{2,1,0:T(2,128)}), f32[128,2,128]{2,1,0:T(2,128)S(1)}, u32[]{:S(2)}, u32[]{:S(2)}) async-start(f32[128,2,128]{2,1,0:T(2,128)} %bitcast.34), calls=%async_computation.4 | async-start | bytes 262144 | tf_op jit(solution)/shard_map/all_to_all | solution.py:479
  94.7 1.4 fusion.7
  96.2 7.9 %all-to-all-done.4 = f32[128,2,128]{2,1,0:T(2,128)S(1)} async-done(((f32[128,2,128]{2,1,0:T(2,128)}), f32[128,2,128]{2,1,0:T(2,128)S(1)}, u32[]{:S(2)}, u32[]{:S(2)}) %all-to-all-start.4) | async-done | bytes 131104 | tf_op jit(solution)/shard_map/all_to_all | solution.py:479
  104.0 0.7 copy-done.10
  104.7 3.1 %columns_third.1 = f32[512,128]{1,0:T(8,128)} custom-call(s32[1]{0:T(128)} %bitcast.refs_0_, bf16[2,256,256]{2,1,0:T(8,128)(2,1)} %constant.44.clone.refs_1_, bf16[2,256,256]{2,1,0:T(8,128)(2,1)} %constant.50.clone.refs_2_, f32[2,128,128]{2,1,0:T(8,128)} %constant.51.clone.refs_3_.refs_0_, bf16[2,256,256]{2,1,0:T(8,128)(2,1)} %constant.48.clone.refs_5_.refs_4_.refs_1_, ...), custom_call_target="tpu_custom_call" | custom-call | tf_op jit(solution)/shard_map/columns_third/pallas_call | solution.py:244
  107.8 5.0 %all-to-all-start.5 = ((f32[128,4,128]{2,1,0:T(4,128)}), f32[128,4,128]{2,1,0:T(4,128)S(1)}, u32[]{:S(2)}, u32[]{:S(2)}) async-start(f32[128,4,128]{2,1,0:T(4,128)} %bitcast.26), calls=%async_computation.5 | async-start | bytes 524288 | tf_op jit(solution)/shard_map/all_to_all | solution.py:479
  112.8 1.1 fusion.9
  113.9 9.4 %all-to-all-done.5 = f32[128,4,128]{2,1,0:T(4,128)S(1)} async-done(((f32[128,4,128]{2,1,0:T(4,128)}), f32[128,4,128]{2,1,0:T(4,128)S(1)}, u32[]{:S(2)}, u32[]{:S(2)}) %all-to-all-start.5) | async-done | bytes 262176 | tf_op jit(solution)/shard_map/all_to_all | solution.py:479
  123.3 0.7 copy-done.6
  124.0 3.2 %rows_finish.1 = (f32[16,2048]{1,0:T(8,128)}, f32[512,128]{1,0:T(8,128)}, f32[64,128]{1,0:T(8,128)}) custom-call(bf16[2,256,256]{2,1,0:T(8,128)(2,1)} %constant.47.clone.refs_4_.refs_0_, bf16[2,256,256]{2,1,0:T(8,128)(2,1)} %constant.48.clone.refs_5_.refs_4_.refs_1_, bf16[2,256,256]{2,1,0:T(8,128)(2,1)} %constant.49.clone.refs_6_.refs_2_, ...), custom_call_target="tpu_custom_call" | custom-call | tf_op jit(solution)/shard_map/rows_finish/pallas_call | solution.py:244
  127.2 4.8 %all-to-all-start.6 = ((f32[128,4,128]{2,1,0:T(4,128)}), f32[128,4,128]{2,1,0:T(4,128)S(1)}, u32[]{:S(2)}, u32[]{:S(2)}) async-start(f32[128,4,128]{2,1,0:T(4,128)} %bitcast.30), calls=%async_computation.6 | async-start | bytes 524288 | tf_op jit(solution)/shard_map/all_to_all | solution.py:479
  132.0 0.0 collective-permute-done
  132.1 3.2 %fusion.5.moved = f32[128,8,256]{2,1,0:T(8,128)S(1)} fusion(f32[128,8,256]{2,1,0:T(8,128)S(1)} %copy-done, f32[128,8,1]{2,1,0:T(8,128)} %get-tuple-element.45, f32[128,8,255]{2,1,0:T(8,128)} %get-tuple-element.47, f32[128,8,255]{2,1,0:T(8,128)} %get-tuple-element.46, f32[128,8,1]{2,1,0:T(8,128)} %get-tuple-element.44, f32[127,8,256]{2,1,0:T(8,128)} %get-tuple-element.41, ...), kind=kLoop, calls=%fused_computation.8 | loop fusion | flops 4456448 | bytes 7340032 | tf_op jit(solution)/shard_map/add | solution.py:466
  135.2 7.3 %all-to-all-done.6 = f32[128,4,128]{2,1,0:T(4,128)S(1)} async-done(((f32[128,4,128]{2,1,0:T(4,128)}), f32[128,4,128]{2,1,0:T(4,128)S(1)}, u32[]{:S(2)}, u32[]{:S(2)}) %all-to-all-start.6) | async-done | bytes 262176 | tf_op jit(solution)/shard_map/all_to_all | solution.py:479
  142.6 0.7 copy-done.5
  143.3 2.7 %columns_slope.1 = f32[768,128]{1,0:T(8,128)} custom-call(s32[1]{0:T(128)} %bitcast.13.refs_0_, bf16[2,512,512]{2,1,0:T(8,128)(2,1)} %constant.53.clone.refs_1_, f32[512,128]{1,0:T(8,128)} %bitcast.22, f32[64,128]{1,0:T(8,128)} %get-tuple-element.37.refs_3_), custom_call_target="tpu_custom_call" | custom-call | tf_op jit(solution)/shard_map/columns_slope/pallas_call | solution.py:244
  146.0 4.7 %all-to-all-start.7 = ((f32[8,96,128]{2,1,0:T(8,128)}), f32[8,96,128]{2,1,0:T(8,128)S(1)}, u32[]{:S(2)}, u32[]{:S(2)}) async-start(f32[8,96,128]{2,1,0:T(8,128)} %bitcast.21), calls=%async_computation.7 | async-start | bytes 786432 | tf_op jit(solution)/shard_map/all_to_all | solution.py:479
  150.7 0.2 fusion.6
  150.9 4.9 %collective-permute-start.3 = (f32[128,2,256]{2,1,0:T(2,128)S(1)}, f32[128,2,256]{2,1,0:T(2,128)S(1)}, u32[]{:S(2)}, u32[]{:S(2)}) collective-permute-start(f32[128,2,256]{2,1,0:T(2,128)S(1)} %get-tuple-element.38), channel_id=1, source_target_pairs={{1,0},{2,1},{3,2},{4,3},{5,4},{6,5},{7,6},{9,8},{10,9},{11,10},{12... | collective-permute-start | bytes 786440 | tf_op jit(solution)/shard_map/ppermute | solution.py:474
  155.7 2.5 %collective-permute-start.2 = (f32[128,2,256]{2,1,0:T(2,128)S(1)}, f32[128,2,256]{2,1,0:T(2,128)S(1)}, u32[]{:S(2)}, u32[]{:S(2)}) collective-permute-start(f32[128,2,256]{2,1,0:T(2,128)S(1)} %get-tuple-element.39), channel_id=1, source_target_pairs={{0,1},{1,2},{2,3},{3,4},{4,5},{5,6},{6,7},{8,9},{9,10},{10,11},{11... | collective-permute-start | bytes 786440 | tf_op jit(solution)/shard_map/ppermute | solution.py:473
  158.2 0.7 pad_add_fusion.place
  158.9 10.9 %collective-permute-done.3.above = f32[128,2,256]{2,1,0:T(2,128)S(1)} collective-permute-done((f32[128,2,256]{2,1,0:T(2,128)S(1)}, f32[128,2,256]{2,1,0:T(2,128)S(1)}, u32[]{:S(2)}, u32[]{:S(2)}) %collective-permute-start.3) | collective-permute-done | bytes 262176 | tf_op jit(solution)/shard_map/ppermute | solution.py:474
  169.8 0.7 copy-done.11
  170.5 0.1 copy-done.12
  170.5 0.1 copy-done.4
  170.7 7.2 %air_finish.1 = f32[128,8,256]{2,1,0:T(8,128)} custom-call(f32[768,128]{1,0:T(8,128)} %bitcast.20, f32[128,8,256]{2,1,0:T(8,128)} %copy-done.1, f32[128,8,256]{2,1,0:T(8,128)} %wind.1, f32[128,2,256]{2,1,0:T(2,128)} %copy-done.12, f32[128,2,256]{2,1,0:T(2,128)} %copy-done.11, s32[2]{0:T(128)} %pad_add_fusion.place), custom_call_target="tpu_custom_call" | custom-call | tf_op jit(solution)/shard_map/air_finish/pallas_call | solution.py:438
  (20 shorter events, 0.0 us)
Async XLA Ops:
  3.8 19.7 %all-to-all-start = ((f32[128,2,128]{2,1,0:T(2,128)}), f32[128,2,128]{2,1,0:T(2,128)S(1)}, u32[]{:S(2)}, u32[]{:S(2)}) async-start(f32[128,2,128]{2,1,0:T(2,128)} %bitcast.33), calls=%async_computation | async-start | bytes 262144 | tf_op jit(solution)/shard_map/all_to_all | solution.py:479
  23.5 0.7 copy-start.9
  27.3 15.3 %all-to-all-start.1 = ((f32[128,4,128]{2,1,0:T(4,128)}), f32[128,4,128]{2,1,0:T(4,128)S(1)}, u32[]{:S(2)}, u32[]{:S(2)}) async-start(f32[128,4,128]{2,1,0:T(4,128)} %bitcast.32), calls=%async_computation.1 | async-start | bytes 524288 | tf_op jit(solution)/shard_map/all_to_all | solution.py:479
  42.6 0.7 copy-start.7
  46.9 15.3 %all-to-all-start.2 = ((f32[128,4,128]{2,1,0:T(4,128)}), f32[128,4,128]{2,1,0:T(4,128)S(1)}, u32[]{:S(2)}, u32[]{:S(2)}) async-start(f32[128,4,128]{2,1,0:T(4,128)} %bitcast.31), calls=%async_computation.2 | async-start | bytes 524288 | tf_op jit(solution)/shard_map/all_to_all | solution.py:479
  62.2 0.7 copy-start.8
  62.9 8.9 %copy-start = (f32[128,8,256]{2,1,0:T(8,128)S(1)}, f32[128,8,256]{2,1,0:T(8,128)}, u32[]{:S(2)}) copy-start(f32[128,8,256]{2,1,0:T(8,128)} %param.17) | copy-start | bytes 3145732
  67.0 18.0 %all-to-all-start.3 = ((f32[128,8,128]{2,1,0:T(8,128)}), f32[128,8,128]{2,1,0:T(8,128)S(1)}, u32[]{:S(2)}, u32[]{:S(2)}) async-start(f32[128,8,128]{2,1,0:T(8,128)} %bitcast.29), calls=%async_computation.3 | async-start | bytes 1048576 | tf_op jit(solution)/shard_map/all_to_all | solution.py:479
  71.8 60.3 %collective-permute-start = (f32[1,8,256]{2,1,0:T(8,128)S(1)}, f32[1,8,256]{2,1,0:T(8,128)S(1)}, u32[]{:S(2)}, u32[]{:S(2)}) collective-permute-start(f32[1,8,256]{2,1,0:T(8,128)S(1)} %get-tuple-element.42), channel_id=1, source_target_pairs={{8,0},{16,8},{24,16},{32,24},{40,32},{48,40},{56,48},{64,56},{72,6... | collective-permute-start | bytes 24584 | tf_op jit(solution)/shard_map/ppermute | solution.py:461
  75.5 56.6 %collective-permute-start.1 = (f32[1,8,256]{2,1,0:T(8,128)S(1)}, f32[1,8,256]{2,1,0:T(8,128)S(1)}, u32[]{:S(2)}, u32[]{:S(2)}) collective-permute-start(f32[1,8,256]{2,1,0:T(8,128)S(1)} %get-tuple-element.43), channel_id=1, source_target_pairs={{0,8},{8,16},{16,24},{24,32},{32,40},{40,48},{48,56},{56,64},{64,7... | collective-permute-start | bytes 24584 | tf_op jit(solution)/shard_map/ppermute | solution.py:460
  85.0 0.8 copy-start.3
  90.1 14.0 %all-to-all-start.4 = ((f32[128,2,128]{2,1,0:T(2,128)}), f32[128,2,128]{2,1,0:T(2,128)S(1)}, u32[]{:S(2)}, u32[]{:S(2)}) async-start(f32[128,2,128]{2,1,0:T(2,128)} %bitcast.34), calls=%async_computation.4 | async-start | bytes 262144 | tf_op jit(solution)/shard_map/all_to_all | solution.py:479
  104.0 0.7 copy-start.10
  107.8 15.5 %all-to-all-start.5 = ((f32[128,4,128]{2,1,0:T(4,128)}), f32[128,4,128]{2,1,0:T(4,128)S(1)}, u32[]{:S(2)}, u32[]{:S(2)}) async-start(f32[128,4,128]{2,1,0:T(4,128)} %bitcast.26), calls=%async_computation.5 | async-start | bytes 524288 | tf_op jit(solution)/shard_map/all_to_all | solution.py:479
  123.3 0.7 copy-start.6
  124.0 8.0 %copy-start.2 = (f32[128,8,256]{2,1,0:T(8,128)S(1)}, f32[128,8,256]{2,1,0:T(8,128)}, u32[]{:S(2)}) copy-start(f32[128,8,256]{2,1,0:T(8,128)} %wind.1) | copy-start | bytes 3145732
  127.2 15.3 %all-to-all-start.6 = ((f32[128,4,128]{2,1,0:T(4,128)}), f32[128,4,128]{2,1,0:T(4,128)S(1)}, u32[]{:S(2)}, u32[]{:S(2)}) async-start(f32[128,4,128]{2,1,0:T(4,128)} %bitcast.30), calls=%async_computation.6 | async-start | bytes 524288 | tf_op jit(solution)/shard_map/all_to_all | solution.py:479
  135.2 15.5 %copy-start.1 = (f32[128,8,256]{2,1,0:T(8,128)}, f32[128,8,256]{2,1,0:T(8,128)S(1)}, u32[]{:S(2)}) copy-start(f32[128,8,256]{2,1,0:T(8,128)S(1)} %fusion.5.moved) | copy-start | bytes 3145732
  142.6 0.7 copy-start.5
  146.0 23.8 %all-to-all-start.7 = ((f32[8,96,128]{2,1,0:T(8,128)}), f32[8,96,128]{2,1,0:T(8,128)S(1)}, u32[]{:S(2)}, u32[]{:S(2)}) async-start(f32[8,96,128]{2,1,0:T(8,128)} %bitcast.21), calls=%async_computation.7 | async-start | bytes 786432 | tf_op jit(solution)/shard_map/all_to_all | solution.py:479
  150.9 18.9 %collective-permute-start.3 = (f32[128,2,256]{2,1,0:T(2,128)S(1)}, f32[128,2,256]{2,1,0:T(2,128)S(1)}, u32[]{:S(2)}, u32[]{:S(2)}) collective-permute-start(f32[128,2,256]{2,1,0:T(2,128)S(1)} %get-tuple-element.38), channel_id=1, source_target_pairs={{1,0},{2,1},{3,2},{4,3},{5,4},{6,5},{7,6},{9,8},{10,9},{11,10},{12... | collective-permute-start | bytes 786440 | tf_op jit(solution)/shard_map/ppermute | solution.py:474
  155.7 14.0 %collective-permute-start.2 = (f32[128,2,256]{2,1,0:T(2,128)S(1)}, f32[128,2,256]{2,1,0:T(2,128)S(1)}, u32[]{:S(2)}, u32[]{:S(2)}) collective-permute-start(f32[128,2,256]{2,1,0:T(2,128)S(1)} %get-tuple-element.39), channel_id=1, source_target_pairs={{0,1},{1,2},{2,3},{3,4},{4,5},{5,6},{6,7},{8,9},{9,10},{10,11},{11... | collective-permute-start | bytes 786440 | tf_op jit(solution)/shard_map/ppermute | solution.py:473
  169.8 0.7 copy-start.11
  169.8 0.8 copy-start.12
  169.8 0.9 copy-start.4

commit v2 on v1

v2 whole, which is shorter than its diff:
```python
import functools

import jax
import jax.numpy as jnp
import ml_dtypes
import numpy as np
from jax import lax
from jax.experimental import pallas as pl
from jax.experimental.pallas import tpu as pltpu
from jax.sharding import PartitionSpec as P

NS = 2048
DT_WAVE = 0.05
COLUMN_DEPTH = 32.0
DT_AIR = 0.1
NU_AIR = 0.2
TWO_PI = 6.283185307179586
WAVE_UNIT = TWO_PI / NS
BOTH = ("gx", "gz")
F32 = jnp.float32
BF16 = jnp.bfloat16


def halves(matrix):
    exact = np.asarray(matrix, np.float64)
    lead = exact.astype(np.float32).astype(ml_dtypes.bfloat16)
    rest = (exact - lead.astype(np.float64)).astype(np.float32).astype(ml_dtypes.bfloat16)
    return np.stack([lead, rest])


@functools.cache
def tables():
    n128, n16 = np.arange(128), np.arange(16)
    eye16, eye8 = np.eye(16), np.eye(8)
    turn = 2 * np.pi * (np.outer(n128, n128) % 128) / 128
    c, s = np.cos(turn), np.sin(turn)
    wheel = np.concatenate([c, s], 0)
    edge = np.zeros((2, 128, 2, 128))
    edge_back = np.zeros((2, 128, 2, 128))
    sign = (-1.0) ** n128
    for d in range(128):
        if d < 64:
            angle, part = 2 * np.pi * n128 * d / 128, 0
        else:
            angle, part = 2 * np.pi * n128 * (2 * (d - 64) + 1) / 256, 1
        edge[0, d, part] = np.cos(angle)
        edge[1, d, part] = -np.sin(angle) if d else sign
        weight = 2.0 if d else 1.0
        edge_back[part, :, 0, d] = weight * np.cos(angle)
        edge_back[part, :, 1, d] = -weight * np.sin(angle) if d else sign
    edge = edge.reshape(256, 256)
    edge_back = edge_back.reshape(256, 256)
    k8 = np.arange(8)
    angle = 2 * np.pi * np.outer(n16, k8) / 16
    near_re, near_im = np.cos(angle), -np.sin(angle)
    near_im[:, 0] = (-1.0) ** n16
    weight = np.where(k8 == 0, 1.0, 2.0)
    near = np.zeros((16, 16, 2, 8, 16))
    near_back = np.zeros((2, 8, 16, 16, 16))
    for part, table in enumerate((near_re, near_im)):
        near[:, :, part] = table[:, None, :, None] * eye16[None, :, None, :]
        near_back[part] = (table * weight).T[:, None, :, None] * eye16[None, :, None, :]
    near = near.reshape(256, 256)
    near_back = near_back.reshape(256, 256)
    angle = 2 * np.pi * np.outer(n16, n16) / 16
    cx, sx = np.kron(eye8, np.cos(angle)), np.kron(eye8, np.sin(angle))
    comb = np.concatenate([cx, sx], 0)
    y_angle = 2 * np.pi * np.repeat(np.outer(n128, k8), 16, axis=1) / NS
    x_angle = 2 * np.pi * np.tile(np.outer(n128, n16), (1, 8)) / NS
    twist = lambda a: np.stack([np.cos(a), -np.sin(a)]).astype(np.float32)
    r = n128[None, :, None, None]
    x = 16 * n128[None, None, :, None] + n16.reshape(4, 1, 1, 4)
    n = r - x
    with np.errstate(divide="ignore", invalid="ignore"):
        slope = np.where(n % NS == 0, 0.0, (np.pi / NS) * (-1.0) ** (n % 2) / np.tan(np.pi * n / NS))
    slope = slope.reshape(512, 512)
    return dict(
        wheel=halves(wheel),
        edge=halves(edge),
        edge_back=halves(edge_back),
        near=halves(near),
        near_back=halves(near_back),
        comb=halves(comb),
        twist_y=twist(y_angle),
        twist_x=twist(x_angle),
        slope=halves(slope),
    )


def dot(a, b):
    return jnp.dot(a, b, preferred_element_type=F32)


def split(x):
    lead = x.astype(BF16)
    return lead, (x - lead.astype(F32)).astype(BF16)


def from_left(table, x):
    lead, rest = split(x)
    width = x.shape[1]
    both = dot(table[0], jnp.concatenate([lead, rest], 1))
    return both[:, :width] + both[:, width:] + dot(table[1], lead)


def from_right(x, table):
    lead, rest = split(x)
    rows = x.shape[0]
    both = dot(jnp.concatenate([lead, rest], 0), table[0])
    return both[:rows] + both[rows:] + dot(lead, table[1])


def turning(table, sign):
    blocks = []
    for half in (table[0], table[1]):
        c, s = half[:128], half[128:]
        upper, lower = (s, -s) if sign > 0 else (-s, s)
        rows = [jnp.concatenate([c, upper], 1), jnp.concatenate([lower, c], 1)]
        blocks.append(jnp.concatenate(rows, 0))
    return blocks


def slot_zero(shape):
    return lax.broadcasted_iota(jnp.int32, shape, 1) % 128 < 16


def y_forward(t, field):
    parts = from_right(field, t["near"])
    re, im = parts[:, :128], parts[:, 128:]
    c, s = t["twist_y"][0], t["twist_y"][1]
    parts = jnp.concatenate([re * c - im * s, re * s + im * c], 0)
    usual = from_left(turning(t["wheel"], 1), parts)
    first = from_left(t["edge"], parts)
    out = jnp.where(slot_zero(usual.shape), first, usual)
    return out[:128], out[128:]


def y_back_far(t, re, im):
    parts = jnp.concatenate([re, im], 0)
    usual = from_left(turning(t["wheel"], -1), parts)
    first = from_left(t["edge_back"], parts)
    parts = jnp.where(slot_zero(usual.shape), first, usual)
    c, s = t["twist_y"][0], t["twist_y"][1]
    out = []
    for at in range(0, parts.shape[1], 128):
        re, im = parts[:128, at : at + 128], parts[128:, at : at + 128]
        out.append(jnp.concatenate([re * c + im * s, im * c - re * s], 1))
    return out


def y_back(t, re, im):
    return from_right(y_back_far(t, re, im)[0], t["near_back"])


def x_forward(t, re, im, mirrored):
    parts = jnp.concatenate([re, im], 0)
    if mirrored:
        parts = jnp.concatenate([parts, jnp.concatenate([re, -im], 0)], 1)
    parts = from_left(turning(t["wheel"], 1), parts)
    c, s = t["twist_x"][0], t["twist_x"][1]
    rows = []
    for at in range(0, parts.shape[1], 128):
        re, im = parts[:128, at : at + 128], parts[128:, at : at + 128]
        rows.append(jnp.concatenate([re * c - im * s, re * s + im * c], 1))
    parts = from_right(jnp.concatenate(rows, 0) if mirrored else rows[0], turning(t["comb"], -1))
    out = parts[:128, :128], parts[:128, 128:]
    if mirrored:
        out += parts[128:, :128], parts[128:, 128:]
    return out


def x_back(t, re, im):
    parts = from_right(jnp.concatenate([re, im], 1), turning(t["comb"], 1))
    re, im = parts[:, :128], parts[:, 128:]
    c, s = t["twist_x"][0], t["twist_x"][1]
    parts = jnp.concatenate([re * c + im * s, im * c - re * s], 0)
    out = from_left(turning(t["wheel"], -1), parts)
    return out[:128], out[128:]


def x_waves():
    q1 = lax.broadcasted_iota(jnp.int32, (128, 128), 0)
    lane = lax.broadcasted_iota(jnp.int32, (128, 128), 1)
    kx = q1 + 128 * (lane % 16)
    return jnp.where(kx < NS // 2, kx, kx - NS)


def odd_x():
    kx = x_waves()
    return jnp.where(kx == -(NS // 2), 0, kx).astype(F32) * WAVE_UNIT


def squared_waves(device):
    slot = lax.broadcasted_iota(jnp.int32, (128, 128), 1) // 16
    first = jnp.where(device < 64, 16 * device, 8 + 16 * (device - 64))
    ky = jnp.where(slot == 0, first, slot + 16 * device)
    other = jnp.where((slot == 0) & (device == 0), NS // 2, ky)
    fold = lambda k: jnp.where(k > NS // 2, NS - k, k).astype(F32) * WAVE_UNIT
    wave_x = x_waves().astype(F32) * WAVE_UNIT
    return wave_x * wave_x + fold(ky) * fold(ky), wave_x * wave_x + fold(other) * fold(other)


def even_filter(spectrum, on_re, on_im):
    re, im, mirror_re, mirror_im = spectrum
    plus = (on_re + on_im) * (0.5 / (NS * NS))
    minus = (on_re - on_im) * (0.5 / (NS * NS))
    return re * plus + mirror_re * minus, im * plus + mirror_im * minus


def power_filter(spectrum, squares, power):
    factors = []
    for square in squares:
        magnitude = jnp.sqrt(square)
        factors.append({1: magnitude, 2: square, 3: square * magnitude}[power])
    return even_filter(spectrum, *factors)


def x_derivative(re, im, scale):
    factor = odd_x() * scale
    return -factor * im, factor * re


def y_derivative(re, im):
    d = lax.broadcasted_iota(jnp.int32, (128, 128), 0)
    slot = lax.broadcasted_iota(jnp.int32, (128, 128), 1) // 16
    first = jnp.where(d < 64, 16 * d, 8 + 16 * (d - 64))
    ky = jnp.where(slot == 0, first, slot + 16 * d)
    factor = jnp.where(ky < NS // 2, ky, ky - NS).astype(F32) * (WAVE_UNIT / NS)
    return -factor * im, factor * re


def to_lanes(rows):
    return jnp.concatenate([rows[:, 128 * a : 128 * a + 128] for a in range(16)], 0).T


def pick(ref, fields, index):
    step = 2 * fields
    return ref[pl.ds(2 * index, 128, step), :], ref[pl.ds(2 * index + 1, 128, step), :]


def put(ref, fields, index, values):
    step = 2 * fields
    ref[pl.ds(2 * index, 128, step), :] = values[0]
    ref[pl.ds(2 * index + 1, 128, step), :] = values[1]


def near_core(array):
    return pltpu.with_memory_space_constraint(array, pltpu.VMEM)


def far_away(array):
    return pltpu.with_memory_space_constraint(array, pltpu.HBM)


def run(body, names, outs, *arrays, held, scalars=None, scratch=(), far=()):
    consts = [near_core(held[name]) for name in names]
    lead = [] if scalars is None else [scalars]
    arrays = [far_away(a) if i in far else near_core(a) for i, a in enumerate(arrays)]

    def kernel(*refs):
        at = len(lead)
        tabs = dict(zip(names, refs[at : at + len(names)]))
        body(tabs, *refs[:at], *refs[at + len(names) :])

    vmem = pl.BlockSpec(memory_space=pltpu.VMEM)
    smem = pl.BlockSpec(memory_space=pltpu.SMEM)
    place = lambda out: (pltpu.VMEM if out[-1] == "near" else pltpu.HBM)(out[:2], F32)
    return pl.pallas_call(
        kernel,
        out_shape=[place(out) for out in outs],
        in_specs=[smem] * len(lead) + [vmem] * (len(consts) + len(arrays)),
        out_specs=[vmem] * len(outs),
        scratch_shapes=list(scratch),
        compiler_params=pltpu.CompilerParams(vmem_limit_bytes=16 << 20),
    )(*lead, *consts, *arrays)


Y_FWD = ("near", "wheel", "edge", "twist_y")
Y_BACK = ("near_back", "wheel", "edge_back", "twist_y")
Y_BOTH = ("near", "wheel", "edge", "twist_y", "near_back", "edge_back")
X_BOTH = ("wheel", "comb", "twist_x")
PLANES = (256, 128)
FIELD = (128, 256, "near")
NAMES = ("wheel", "comb", "twist_x", "near", "near_back", "edge", "edge_back", "twist_y")


def copied(names, arrays, body, outs, keep):
    sources = [jnp.asarray(tables()[name]) for name in names] + list(arrays)
    count, kept = len(sources), len(names) if keep else 0

    def kernel(*refs):
        sems = refs[-1]
        inputs, results = refs[:count], refs[count : count + len(outs)]
        targets = refs[count + len(outs) : -1]
        copies = [pltpu.make_async_copy(inputs[i], targets[i], sems.at[i]) for i in range(count)]
        for copy in copies:
            copy.start()
        for copy in copies:
            copy.wait()
        if body is not None:
            body(dict(zip(names, targets)), *targets[len(names) :], *results)

    vmem = pl.BlockSpec(memory_space=pltpu.VMEM)
    return pl.pallas_call(
        kernel,
        out_shape=[pltpu.HBM(out[:2], F32) for out in outs]
        + [pltpu.VMEM(c.shape, c.dtype) for c in sources[:kept]],
        in_specs=[pl.BlockSpec(memory_space=pltpu.HBM)] * count,
        out_specs=[vmem] * (len(outs) + kept),
        scratch_shapes=[pltpu.VMEM(c.shape, c.dtype) for c in sources[kept:]]
        + [pltpu.SemaphoreType.DMA((count,))],
        compiler_params=pltpu.CompilerParams(vmem_limit_bytes=16 << 20),
    )(*[far_away(source) for source in sources])


def hold_tables():
    return dict(zip(NAMES, copied(NAMES, (), None, (), True)))


def stacked(ref):
    return [ref[128 * i : 128 * i + 128, :] for i in range(ref.shape[0] // 128)]


def rows_start(t, phi, send):
    put(send, 1, 0, y_forward(t, to_lanes(phi[...])))


def rows_surface(t, eta, start, send, lanes, slope, speed):
    lanes[...] = to_lanes(eta[...])
    spectrum = y_forward(t, lanes[...])
    put(send, 1, 0, spectrum)
    slope[...] = y_back(t, *y_derivative(*spectrum))
    speed[...] = y_back(t, *y_derivative(*pick(start, 1, 0)))


def columns_first(t, device, got, send, held):
    spectrum = x_forward(t, *pick(got, 1, 0), True)
    for i, part in enumerate(spectrum):
        held[128 * i : 128 * i + 128, :] = part
    put(send, 1, 0, x_back(t, *power_filter(spectrum, squared_waves(device[0]), 1)))


def columns_first_late(t, device, held, late):
    spectrum = stacked(held)
    squares = squared_waves(device[0])
    put(late, 3, 0, x_back(t, *power_filter(spectrum, squares, 2)))
    put(late, 3, 1, x_back(t, *power_filter(spectrum, squares, 3)))
    put(late, 3, 2, x_back(t, *x_derivative(spectrum[0], spectrum[1], 1.0 / (NS * NS))))


def rows_second(t, got, lanes, surface, send, once):
    once[...] = y_back(t, *pick(got, 1, 0))
    put(send, 2, 0, y_forward(t, -lanes[...] * once[...]))
    put(send, 2, 1, pick(surface, 1, 0))


def columns_second(t, device, got, late, send, held):
    spectrum = x_forward(t, *pick(got, 2, 0), True)
    for i, part in enumerate(spectrum):
        held[128 * i : 128 * i + 128, :] = part
    for i, part in enumerate(pick(got, 2, 1)):
        held[512 + 128 * i : 640 + 128 * i, :] = part
    put(send, 4, 0, x_back(t, *power_filter(spectrum, squared_waves(device[0]), 1)))
    for index in range(3):
        put(send, 4, 1 + index, pick(late, 3, index))


def columns_second_late(t, device, held, late):
    parts = stacked(held)
    put(late, 2, 0, x_back(t, *power_filter(parts[:4], squared_waves(device[0]), 2)))
    re, im = x_forward(t, parts[4], parts[5], False)
    put(late, 2, 1, x_back(t, *x_derivative(re, im, 1.0 / (NS * NS))))


def rows_third(t, got, lanes, send, once, twice):
    eta = lanes[...]
    once[...] = y_back(t, *pick(got, 4, 0))
    twice[...] = y_back(t, *pick(got, 4, 1))
    third = -eta * once[...] - 0.5 * eta * eta * twice[...]
    put(send, 1, 0, y_forward(t, third))


def rows_third_late(t, got, lanes, first_once, once, twice, sums, speed):
    eta = lanes[...]
    thrice = y_back(t, *pick(got, 4, 2))
    speed[...] = y_back(t, *pick(got, 4, 3))
    sums[...] = first_once[...] + eta * twice[...] + 0.5 * eta * eta * thrice + once[...]


def columns_third(t, device, got, late, send):
    spectrum = x_forward(t, *pick(got, 1, 0), True)
    put(send, 3, 0, x_back(t, *power_filter(spectrum, squared_waves(device[0]), 1)))
    for index in range(2):
        put(send, 3, 1 + index, pick(late, 2, index))


def finished(t, parts, lanes, sums, speed_x, speed_y, slope_y, width):
    near = [half[:, :width] for half in (t["near_back"][0], t["near_back"][1])]
    back = from_right(jnp.concatenate(parts, 0), near)
    third_once, second_twice, slope_x = back[:128], back[128:256], back[256:]
    eta, along = lanes[:, :width], slope_y[:, :width]
    tendency = -(slope_x * speed_x[:, :width] + along * speed_y[:, :width]) + (
        1.0 + slope_x * slope_x + along * along
    ) * (sums[:, :width] + third_once + eta * second_twice)
    return eta + DT_WAVE * tendency


def rows_finish(t, got, lanes, sums, speed_x, speed_y, slope_y, parts_out, send, window):
    parts = y_back_far(t, *[jnp.concatenate(p, 1) for p in zip(*[pick(got, 3, i) for i in range(3)])])
    for i, part in enumerate(parts):
        parts_out[128 * i : 128 * i + 128, :] = part
    new = finished(t, parts, lanes, sums, speed_x, speed_y, slope_y, 128).T[:32]
    window[0:32, :] = new
    window[32:64, :] = lanes[:, 0:128].T[:32]
    group = lax.broadcasted_iota(jnp.int32, (16, 128), 1) // 32
    blocks = []
    for a in range(2):
        rows = new[16 * a : 16 * a + 16]
        turned = [rows] + [pltpu.roll(rows, 32 * k, 1) for k in range(1, 4)]
        for chunk in range(4):
            block = jnp.zeros((4, 128), F32)
            for g in range(4):
                moved = turned[(g - chunk) % 4]
                block = block + jnp.where(group == g, moved, 0.0)[4 * g : 4 * g + 4]
            blocks.append(block)
    block = jnp.concatenate(blocks, 0)
    for at in range(16):
        send[32 * at : 32 * at + 32, :] = block


def rows_output(t, parts, lanes, sums, speed_x, speed_y, slope_y, new_rows):
    parts = [parts[128 * i : 128 * i + 128, :] for i in range(3)]
    new = finished(t, parts, lanes, sums, speed_x, speed_y, slope_y, 256).T
    for a in range(16):
        new_rows[:, 128 * a : 128 * a + 128] = new[16 * a : 16 * a + 16]


def columns_slope(t, slab, got, window, table, send, twofold):
    twofold[0:512, :] = got[...]
    twofold[512:1024, :] = got[...]
    start = pl.multiple_of(slab[0] * 32, 32)
    full = from_left(table, twofold[pl.ds(start, 512), :])
    group = lax.broadcasted_iota(jnp.int32, (128, 128), 1) // 32
    total = jnp.zeros((128, 128), F32)
    for g in range(4):
        total = total + jnp.where(group == g, full[128 * g : 128 * g + 128], 0.0)
    total = total + pltpu.roll(total, 64, 1)
    total = total + pltpu.roll(total, 32, 1)
    slope = total.T[:32]
    for at in range(8):
        send[96 * at : 96 * at + 32, :] = slope
        send[96 * at + 32 : 96 * at + 96, :] = window[...]


def air_moved(t, tracer, wind, before, after, moved, bottom, top):
    levels = before.shape[0]
    count = tracer.shape[0] // levels
    lane = lax.broadcasted_iota(jnp.int32, (levels, 256), 1)

    def put_row(x, west, east):
        at = at_row(x)
        q, w = tracer[at, :], wind[at, :]
        north = jnp.where(lane == 255, q, pltpu.roll(q, 255, 1))
        south = jnp.where(lane == 0, q, pltpu.roll(q, 1, 1))
        q = q + DT_AIR * (
            -w * (east - west) * 0.5 + NU_AIR * (east + west + north + south - 4.0 * q)
        )
        moved[at, :] = q
        for k in range(2):
            bottom[pl.ds(128 * k + x, 1), :] = q[k : k + 1]
            top[pl.ds(128 * k + x, 1), :] = q[levels - 2 + k : levels - 1 + k]

    def at_row(x):
        return pl.ds(pl.multiple_of(x * levels, levels), levels)

    put_row(0, before[...], tracer[at_row(1), :])
    put_row(count - 1, tracer[at_row(count - 2), :], after[...])

    def step(i, carry):
        for k in range(6):
            x = 1 + 6 * i + k
            put_row(x, tracer[at_row(x - 1), :], tracer[at_row(x + 1), :])
        return carry

    lax.fori_loop(0, (count - 2) // 6, step, 0)


def air_finish(place, got, moved, wind, below, above, lowest_rows, highest_rows, out, *scratch):
    ratio_s, inverse_s, spread_s, low_s, high_s, r_low_s, r_high_s = scratch
    block = pl.program_id(0)
    levels = 8
    depth = out.shape[0] // levels
    group, groups = place[0], place[1]
    total = (levels * groups).astype(F32)
    bottom, top = group == 0, group == groups - 1

    def lift_of(level):
        return 1.0 - ((group * levels + level).astype(F32) + 0.5) / total

    def remap(lower, mid, upper, shift):
        return (
            mid + 0.5 * shift * (upper - lower) + 0.5 * shift * shift * (upper - 2.0 * mid + lower)
        )

    @pl.when(block == 0)
    def _():
        slope = jnp.concatenate([got[96 * g : 96 * g + 32, :] for g in range(8)], 0).T
        for g in range(8):
            for a in range(2):
                at = 96 * g + 32 + 16 * a
                rows, lanes = slice(16 * g, 16 * g + 16), slice(128 * a, 128 * a + 128)
                new, old = got[at : at + 16, :], got[at + 32 : at + 48, :]
                ratio_s[rows, lanes] = (new - old) / (COLUMN_DEPTH - old) * total
                inverse = 1.0 / (COLUMN_DEPTH - new)
                inverse_s[rows, lanes] = inverse * (DT_AIR * 0.5 * total) * slope[rows, lanes]
                spread_s[rows, lanes] = inverse * inverse * (DT_AIR * NU_AIR * total * total)
        first, last = lowest_rows[0:128, :], highest_rows[128:256, :]
        low = jnp.where(bottom, first, below[128:256, :])
        high = jnp.where(top, last, above[0:128, :])
        low_s[...], high_s[...] = low, high
        shift = ratio_s[...]
        r_low_s[...] = remap(below[0:128, :], low, first, shift * lift_of(jnp.int32(-1)))
        r_high_s[...] = remap(last, high, above[128:256, :], shift * lift_of(jnp.int32(levels)))

    level = lax.broadcasted_iota(jnp.int32, (levels, 256), 0)
    lift = lift_of(level)
    lowest, highest = level == 0, level == levels - 1

    def step(i, carry):
        for k in range(4):
            x = 4 * i + k
            row = pl.ds(block * depth + x, 1)
            at = pl.ds(pl.multiple_of(x * levels, levels), levels)
            m = moved[at, :]
            lower = jnp.where(lowest, low_s[row, :], pltpu.roll(m, 1, 0))
            upper = jnp.where(highest, high_s[row, :], pltpu.roll(m, levels - 1, 0))
            r = remap(lower, m, upper, ratio_s[row, :] * lift)
            r_low = jnp.where(bottom, r[:1], r_low_s[row, :])
            r_high = jnp.where(top, r[levels - 1 :], r_high_s[row, :])
            lower = jnp.where(lowest, r_low, pltpu.roll(r, 1, 0))
            upper = jnp.where(highest, r_high, pltpu.roll(r, levels - 1, 0))
            out[at, :] = (
                r
                + spread_s[row, :] * (upper - 2.0 * r + lower)
                + wind[at, :] * lift * inverse_s[row, :] * (upper - lower)
            )
        return carry

    lax.fori_loop(0, depth // 4, step, 0)


def air_finish_call(place, got, moved, wind, below, above, bottom, top):
    depth = 16
    rows = pl.BlockSpec((8 * depth, 256), lambda i: (i, 0))
    whole = lambda shape: pl.BlockSpec(shape, lambda i: (0, 0))
    rim = whole((256, 256))
    return pl.pallas_call(
        air_finish,
        out_shape=jax.ShapeDtypeStruct(moved.shape, F32),
        grid=(128 // depth,),
        in_specs=[
            pl.BlockSpec(memory_space=pltpu.SMEM),
            whole((768, 128)),
            rows,
            rows,
            rim,
            rim,
            rim,
            rim,
        ],
        out_specs=rows,
        scratch_shapes=[pltpu.VMEM((128, 256), F32)] * 7,
        compiler_params=pltpu.CompilerParams(vmem_limit_bytes=16 << 20),
        name="air_finish",
    )(place, got, moved, wind, below, above, bottom, top)


def exchange(buffer, axes=BOTH, fields=1):
    if fields == 3:
        buffer = buffer.reshape(128, 3, 2, 128)
    out = lax.all_to_all(buffer, axes, split_axis=0, concat_axis=0, tiled=True)
    return out.reshape(-1, 128)


def shards(elevation, potential, tracer, wind_speed):
    gx, gz = lax.axis_index("gx"), lax.axis_index("gz")
    groups = lax.axis_size("gz")
    device = (gx * groups + gz).astype(jnp.int32).reshape(1)
    slab = gx.astype(jnp.int32).reshape(1)
    place = jnp.concatenate([gz.astype(jnp.int32).reshape(1), jnp.full((1,), groups, jnp.int32)])
    quantity = tracer.reshape(1024, 256)
    wind = wind_speed.reshape(1024, 256)
    size = lax.axis_size("gx")
    ring = [(i, (i + 1) % size) for i in range(size)]
    rise = [(i, i + 1) for i in range(groups - 1)]
    back = lambda pairs: [(j, i) for i, j in pairs]

    (start,) = copied(Y_FWD, [potential], rows_start, [PLANES], False)
    got = exchange(start)
    t = hold_tables()
    surface, lanes, slope_y, speed_y = run(
        rows_surface,
        Y_BOTH,
        [(256, 128, "near"), FIELD, FIELD, FIELD],
        elevation,
        start,
        held=t,
        far=(0, 1),
    )

    send, held = run(
        columns_first, X_BOTH, [PLANES, (512, 128, "near")], got, scalars=device, held=t
    )
    got = exchange(send)
    (late,) = run(columns_first_late, X_BOTH, [(768, 128, "near")], held, scalars=device, held=t)
    before = lax.ppermute(quantity[-8:], "gx", ring)
    after = lax.ppermute(quantity[:8], "gx", back(ring))

    send, first_once = run(rows_second, Y_BOTH, [(512, 128), FIELD], got, lanes, surface, held=t)
    got = exchange(send)
    moved, bottom, top = run(
        air_moved,
        (),
        [(1024, 256), (256, 256), (256, 256)],
        quantity,
        wind,
        before,
        after,
        held=t,
        far=(0, 1, 2, 3),
    )

    send, held = run(
        columns_second,
        X_BOTH,
        [(1024, 128), (768, 128, "near")],
        got,
        late,
        scalars=device,
        held=t,
    )
    got = exchange(send)
    (late,) = run(columns_second_late, X_BOTH, [(512, 128, "near")], held, scalars=device, held=t)
    below = lax.ppermute(top, "gz", rise)
    above = lax.ppermute(bottom, "gz", back(rise))

    send, once, twice = run(rows_third, Y_BOTH, [PLANES, FIELD, FIELD], got, lanes, held=t)
    got_rows, got = got, exchange(send)
    sums, speed_x = run(
        rows_third_late,
        Y_BACK,
        [FIELD, FIELD],
        got_rows,
        lanes,
        first_once,
        once,
        twice,
        held=t,
    )

    (send,) = run(columns_third, X_BOTH, [(768, 128)], got, late, scalars=device, held=t)
    got = exchange(send, fields=3)

    surface_set = (lanes, sums, speed_x, speed_y, slope_y)
    parts, send, window = run(
        rows_finish,
        Y_BACK,
        [(384, 256, "near"), (512, 128), (64, 128, "near")],
        got,
        *surface_set,
        held=t,
    )
    got = exchange(send)
    (new_rows,) = run(
        rows_output, ("near_back",), [(16, NS)], parts, *surface_set, held=t
    )
    (send,) = run(
        columns_slope,
        (),
        [(768, 128)],
        got,
        window,
        jnp.asarray(tables()["slope"]),
        scalars=slab,
        held=t,
        scratch=[pltpu.VMEM((1024, 128), F32)],
    )
    got = exchange(send, "gz")
    out = air_finish_call(place, got, moved, wind, below, above, bottom, top)
    return new_rows, out.reshape(tracer.shape)


def solution(mesh):
    return jax.shard_map(
        shards,
        mesh=mesh,
        in_specs=(P(BOTH, None), P(BOTH, None), P("gx", "gz", None), P("gx", "gz", None)),
        out_specs=(P(BOTH, None), P("gx", "gz", None)),
        check_vma=False,
    )
```

time: 179 us -> 171 us (0.955)
  blocking collectives: 0 us -> 33.9 us
  waiting for transfers between devices: 67.9 us -> 52.2 us
  starting transfers between devices: 54.9 us -> 46.4 us
  Pallas kernels: 40.1 us -> 32 us
  local copies, waits for them, and re-layouts: 10.3 us -> 5.15 us
  other arithmetic: 3.82 us -> 0.08 us
    all_to_all x0 -> x2, blocking collectives: none -> 33.9 us  [exchange(): out = lax.all_to_all(buffer, axes, split_axis=0, concat_axis=0, tiled=True)]
    all_to_all x8 -> x6, waiting for transfers between devices: 57 us -> 43.4 us  [exchange(): out = lax.all_to_all(buffer, axes, split_axis=0, concat_axis=0, tiled=True)]
    all_to_all x8 -> x6, starting transfers between devices: 43.9 us -> 34.2 us  [exchange(): out = lax.all_to_all(buffer, axes, split_axis=0, concat_axis=0, tiled=True)]
    pallas_call x11 -> x16, Pallas kernels: 40.1 us -> 32 us  [the longest x13 23.6 us: run(): pl.pallas_call(kernel, out_shape=[place(out) for out in outs], in_specs=[...]
    slice x5 -> x1, local copies, waits for them, and re-layouts: 4.41 us -> 0.72 us  [shards(): after = lax.ppermute(quantity[:8], 'gx', back(ring))]
    add x1 -> x0, other arithmetic: 3.16 us -> none  [moved_air(): tracer + DT_AIR * (-wind_speed * (eastern - western) * 0.5 + NU_AIR * (ea...]
    ppermute x4, waiting for transfers between devices: 10.9 us -> 8.84 us  [the longest x1 5.93 us: shards(): below = lax.ppermute(top, 'gz', rise)]
    unnamed x26 -> x18, local copies, waits for them, and re-layouts: 5.87 us -> 4.44 us
  transfers between devices with their start and end apart: 12 -> 10, of which waited for: 8 -> 8; matrix products, arithmetic and copies ran while one was open for 5% -> 0% of each run, Pallas kernels for 9% -> 8%
where the time goes in v2:
time: 171 us
  waiting for transfers between devices  52.2 us (31%)
  starting transfers between devices  46.4 us (27%)
  blocking collectives  33.9 us (20%)
  Pallas kernels  32 us (19%)
  local copies, waits for them, and re-layouts  5.15 us (3%)
    all_to_all x6, waiting for transfers between devices, exchange(): out = lax.all_to_all(buffer, axes, split_axis=0, concat_axis=0, tiled=True)  43.4 us
    all_to_all x6, starting transfers between devices, exchange(): out = lax.all_to_all(buffer, axes, split_axis=0, concat_axis=0, tiled=True)  34.2 us
    all_to_all x2, blocking collectives, exchange(): out = lax.all_to_all(buffer, axes, split_axis=0, concat_axis=0, tiled=True)  33.9 us
    pallas_call x13, Pallas kernels, run(): pl.pallas_call(kernel, out_shape=[place(out) for out in outs], in_specs=[...  23.6 us
    ppermute x1, waiting for transfers between devices, shards(): below = lax.ppermute(top, 'gz', rise)  5.93 us
    ppermute x1, starting transfers between devices, shards(): below = lax.ppermute(top, 'gz', rise)  5.02 us
    unnamed x18, local copies, waits for them, and re-layouts  4.44 us
    pallas_call x1, Pallas kernels, air_finish_call(): pl.pallas_call(air_finish, out_shape=jax.ShapeDtypeStruct(moved.shape, F3...  4.41 us
  transfers between devices with their start and end apart: 10, of which 8 were waited for; matrix products, arithmetic and copies ran while one was open for 0% of the time, Pallas kernels for 8%

profile of v2, /device:TPU:8, one launch (start us, length us, event | category | flops | bytes accessed | tf_op | source)
XLA Modules:
  0.0 170.5 jit_solution(9079947045620131126)
XLA Ops:
  0.6 2.5 %shard_map.141.refs_7_ = f32[256,128]{1,0:T(8,128)} custom-call(bf16[2,256,256]{2,1,0:T(8,128)(2,1)} %constant.31.clone.refs_3_.refs_0_, bf16[2,256,128]{2,1,0:T(8,128)(2,1)} %constant.32.clone.refs_0_.refs_1_, bf16[2,256,256]{2,1,0:T(8,128)(2,1)} %constant.33.clone.refs_5_.refs_2_, f32[2,128,128]{2,1,0:T(8,128)} %constant.34.clone.refs_7_.refs_3_, ...), custom_call_target="tpu_custom_call" | custom-call | tf_op jit(solution)/shard_map/pallas_call | solution.py:304
  3.1 10.4 %all-to-all-start = ((f32[128,2,128]{2,1,0:T(2,128)}), f32[128,2,128]{2,1,0:T(2,128)S(1)}, u32[]{:S(2)}, u32[]{:S(2)}) async-start(f32[128,2,128]{2,1,0:T(2,128)} %bitcast.39), calls=%async_computation | async-start | bytes 262144 | tf_op jit(solution)/shard_map/all_to_all | solution.py:581
  13.6 1.5 shard_map.140
  15.1 7.7 %all-to-all-done = f32[128,2,128]{2,1,0:T(2,128)S(1)} async-done(((f32[128,2,128]{2,1,0:T(2,128)}), f32[128,2,128]{2,1,0:T(2,128)S(1)}, u32[]{:S(2)}, u32[]{:S(2)}) %all-to-all-start) | async-done | bytes 131104 | tf_op jit(solution)/shard_map/all_to_all | solution.py:581
  22.8 1.8 %shard_map.142 = (f32[256,128]{1,0:T(8,128)}, f32[512,128]{1,0:T(8,128)S(1)}) custom-call(s32[1]{0:T(128)} %bitcast.refs_0_, bf16[2,256,128]{2,1,0:T(8,128)(2,1)S(1)} %get-tuple-element.32.refs_1_, bf16[2,256,128]{2,1,0:T(8,128)(2,1)S(1)} %get-tuple-element.35.refs_2_, f32[2,128,128]{2,1,0:T(8,128)S(1)} %get-tuple-element.36.refs_3_, f32[256,128]{1,0:T(8,128)S(1)} %bitcast.34), custom_call_target="tpu_custom_call" | custom-call | tf_op jit(solution)/shard_map/pallas_call | solution.py:268
  24.6 4.8 %all-to-all-start.1 = ((f32[128,2,128]{2,1,0:T(2,128)}), f32[128,2,128]{2,1,0:T(2,128)S(1)}, u32[]{:S(2)}, u32[]{:S(2)}) async-start(f32[128,2,128]{2,1,0:T(2,128)} %bitcast.45), calls=%async_computation.1 | async-start | bytes 262144 | tf_op jit(solution)/shard_map/all_to_all | solution.py:581
  29.4 2.4 %shard_map.143 = (f32[256,128]{1,0:T(8,128)S(1)}, f32[128,256]{1,0:T(8,128)S(1)}, f32[128,256]{1,0:T(8,128)S(1)}, f32[128,256]{1,0:T(8,128)S(1)}) custom-call(bf16[2,256,256]{2,1,0:T(8,128)(2,1)S(1)} %get-tuple-element.37.refs_0_, bf16[2,256,128]{2,1,0:T(8,128)(2,1)S(1)} %get-tuple-element.32.refs_1_, bf16[2,256,256]{2,1,0:T(8,128)(2,1)S(1)} %get-tuple-element.38.refs_2_, ...), custom_call_target="tpu_custom_call" | custom-call | tf_op jit(solution)/shard_map/pallas_call | solution.py:268
  31.8 6.9 %all-to-all-done.1 = f32[128,2,128]{2,1,0:T(2,128)S(1)} async-done(((f32[128,2,128]{2,1,0:T(2,128)}), f32[128,2,128]{2,1,0:T(2,128)S(1)}, u32[]{:S(2)}, u32[]{:S(2)}) %all-to-all-start.1) | async-done | bytes 131104 | tf_op jit(solution)/shard_map/all_to_all | solution.py:581
  38.7 1.7 shard_map.144
  40.3 4.8 %all-to-all-start.2 = ((f32[128,4,128]{2,1,0:T(4,128)}), f32[128,4,128]{2,1,0:T(4,128)S(1)}, u32[]{:S(2)}, u32[]{:S(2)}) async-start(f32[128,4,128]{2,1,0:T(4,128)} %bitcast.43), calls=%async_computation.2 | async-start | bytes 524288 | tf_op jit(solution)/shard_map/all_to_all | solution.py:581
  45.1 0.9 shard_map.145.refs_5_
  46.1 9.6 %all-to-all-done.2 = f32[128,4,128]{2,1,0:T(4,128)S(1)} async-done(((f32[128,4,128]{2,1,0:T(4,128)}), f32[128,4,128]{2,1,0:T(4,128)S(1)}, u32[]{:S(2)}, u32[]{:S(2)}) %all-to-all-start.2) | async-done | bytes 262176 | tf_op jit(solution)/shard_map/all_to_all | solution.py:581
  55.7 1.9 %shard_map.146 = (f32[1024,128]{1,0:T(8,128)}, f32[768,128]{1,0:T(8,128)S(1)}) custom-call(s32[1]{0:T(128)} %bitcast.refs_0_, bf16[2,256,128]{2,1,0:T(8,128)(2,1)S(1)} %get-tuple-element.32.refs_1_, bf16[2,256,128]{2,1,0:T(8,128)(2,1)S(1)} %get-tuple-element.35.refs_2_, f32[2,128,128]{2,1,0:T(8,128)S(1)} %get-tuple-element.36.refs_3_, ...), custom_call_target="tpu_custom_call" | custom-call | tf_op jit(solution)/shard_map/pallas_call | solution.py:268
  57.6 18.2 %all_to_all.82 = f32[128,8,128]{2,1,0:T(8,128)S(1)} all-to-all(f32[128,8,128]{2,1,0:T(8,128)} %bitcast.42), channel_id=1, replica_groups=mesh['gx'=16,'gz'=8] {'gx','gz'}, dimensions={0} | all-to-all | bytes 1048576 | tf_op jit(solution)/shard_map/all_to_all | solution.py:581
  75.8 1.9 %shard_map.147 = (f32[256,128]{1,0:T(8,128)}, f32[128,256]{1,0:T(8,128)S(1)}, f32[128,256]{1,0:T(8,128)S(1)}) custom-call(bf16[2,256,256]{2,1,0:T(8,128)(2,1)S(1)} %get-tuple-element.37.refs_0_, bf16[2,256,128]{2,1,0:T(8,128)(2,1)S(1)} %get-tuple-element.32.refs_1_, bf16[2,256,256]{2,1,0:T(8,128)(2,1)S(1)} %get-tuple-element.38.refs_2_, ...), custom_call_target="tpu_custom_call" | custom-call | tf_op jit(solution)/shard_map/pallas_call | solution.py:268
  77.7 4.7 %all-to-all-start.4 = ((f32[128,2,128]{2,1,0:T(2,128)}), f32[128,2,128]{2,1,0:T(2,128)S(1)}, u32[]{:S(2)}, u32[]{:S(2)}) async-start(f32[128,2,128]{2,1,0:T(2,128)} %bitcast.46), calls=%async_computation.4 | async-start | bytes 262144 | tf_op jit(solution)/shard_map/all_to_all | solution.py:581
  82.4 1.2 shard_map.148.refs_5_
  83.7 8.1 %all-to-all-done.4 = f32[128,2,128]{2,1,0:T(2,128)S(1)} async-done(((f32[128,2,128]{2,1,0:T(2,128)}), f32[128,2,128]{2,1,0:T(2,128)S(1)}, u32[]{:S(2)}, u32[]{:S(2)}) %all-to-all-start.4) | async-done | bytes 131104 | tf_op jit(solution)/shard_map/all_to_all | solution.py:581
  91.8 1.8 %shard_map.149 = f32[768,128]{1,0:T(8,128)} custom-call(s32[1]{0:T(128)} %bitcast.refs_0_, bf16[2,256,128]{2,1,0:T(8,128)(2,1)S(1)} %get-tuple-element.32.refs_1_, bf16[2,256,128]{2,1,0:T(8,128)(2,1)S(1)} %get-tuple-element.35.refs_2_, f32[2,128,128]{2,1,0:T(8,128)S(1)} %get-tuple-element.36.refs_3_, f32[256,128]{1,0:T(8,128)S(1)} %bitcast.35, ...), custom_call_target="tpu_custom_call" | custom-call | tf_op jit(solution)/shard_map/pallas_call | solution.py:268
  93.6 4.8 %all-to-all-start.5 = ((f32[128,3,2,128]{3,2,1,0:T(2,128)}), f32[128,3,2,128]{3,2,1,0:T(2,128)S(1)}, u32[]{:S(2)}, u32[]{:S(2)}) async-start(f32[128,3,2,128]{3,2,1,0:T(2,128)} %bitcast.38), calls=%async_computation.5 | async-start | bytes 786432 | tf_op jit(solution)/shard_map/all_to_all | solution.py:581
  98.4 0.8 shard_map.150
  99.2 11.1 %all-to-all-done.5 = f32[128,3,2,128]{3,2,1,0:T(2,128)S(1)} async-done(((f32[128,3,2,128]{3,2,1,0:T(2,128)}), f32[128,3,2,128]{3,2,1,0:T(2,128)S(1)}, u32[]{:S(2)}, u32[]{:S(2)}) %all-to-all-start.5) | async-done | bytes 393248 | tf_op jit(solution)/shard_map/all_to_all | solution.py:581
  110.2 1.7 shard_map.151
  111.9 15.7 %all_to_all.83 = f32[128,4,128]{2,1,0:T(4,128)S(1)} all-to-all(f32[128,4,128]{2,1,0:T(4,128)} %bitcast.44), channel_id=1, replica_groups=mesh['gx'=16,'gz'=8] {'gx','gz'}, dimensions={0} | all-to-all | bytes 524288 | tf_op jit(solution)/shard_map/all_to_all | solution.py:581
  127.6 0.0 copy-done.2
  127.6 1.4 shard_map.153
  129.0 4.7 %all-to-all-start.7 = ((f32[8,96,128]{2,1,0:T(8,128)}), f32[8,96,128]{2,1,0:T(8,128)S(1)}, u32[]{:S(2)}, u32[]{:S(2)}) async-start(f32[8,96,128]{2,1,0:T(8,128)} %bitcast.37), calls=%async_computation.7 | async-start | bytes 786432 | tf_op jit(solution)/shard_map/all_to_all | solution.py:581
  133.7 0.7 slice_bitcast_fusion
  134.4 0.0 collective-permute-start
  134.4 3.9 %collective-permute-start.1 = (f32[8,256]{1,0:T(8,128)S(1)}, f32[8,256]{1,0:T(8,128)S(1)}, u32[]{:S(2)}, u32[]{:S(2)}) collective-permute-start(f32[8,256]{1,0:T(8,128)S(1)} %get-tuple-element.60), channel_id=1, source_target_pairs={{8,0},{16,8},{24,16},{32,24},{40,32},{48,40},{56,48},{64,56},{72,6... | collective-permute-start | bytes 24584 | tf_op jit(solution)/shard_map/ppermute | solution.py:617
  138.3 1.4 collective-permute-done.refs_2_
  139.7 0.0 collective-permute-done.1.refs_3_
  139.7 0.6 copy-done.7
  140.3 5.0 %shard_map.154 = (f32[1024,256]{1,0:T(8,128)}, f32[256,256]{1,0:T(8,128)}, f32[256,256]{1,0:T(8,128)}) custom-call(f32[1024,256]{1,0:T(8,128)} %bitcast.40, f32[1024,256]{1,0:T(8,128)} %bitcast.28, f32[8,256]{1,0:T(8,128)} %copy-done.7, f32[8,256]{1,0:T(8,128)} %copy-done.8), custom_call_target="tpu_custom_call" | custom-call | tf_op jit(solution)/shard_map/pallas_call | solution.py:268
  145.3 5.0 %collective-permute-start.2 = (f32[256,256]{1,0:T(8,128)}, f32[256,256]{1,0:T(8,128)S(1)}, u32[]{:S(2)}, u32[]{:S(2)}) collective-permute-start(f32[256,256]{1,0:T(8,128)} %get-tuple-element.58.highest_rows), channel_id=1, source_target_pairs={{0,1},{1,2},{2,3},{3,4},{4,5},{5,6},{6,7},{8,9},{9,10},{10,11},{11... | collective-permute-start | bytes 786440 | tf_op jit(solution)/shard_map/ppermute | solution.py:644
  150.3 3.3 %collective-permute-start.3 = (f32[256,256]{1,0:T(8,128)}, f32[256,256]{1,0:T(8,128)S(1)}, u32[]{:S(2)}, u32[]{:S(2)}) collective-permute-start(f32[256,256]{1,0:T(8,128)} %get-tuple-element.59.lowest_rows), channel_id=1, source_target_pairs={{1,0},{2,1},{3,2},{4,3},{5,4},{6,5},{7,6},{9,8},{10,9},{11,10},{12... | collective-permute-start | bytes 786440 | tf_op jit(solution)/shard_map/ppermute | solution.py:645
  153.7 0.1 pad_add_fusion.place
  153.7 1.1 shard_map.152
  154.8 5.9 %collective-permute-done.2.below = f32[256,256]{1,0:T(8,128)S(1)} collective-permute-done((f32[256,256]{1,0:T(8,128)}, f32[256,256]{1,0:T(8,128)S(1)}, u32[]{:S(2)}, u32[]{:S(2)}) %collective-permute-start.2) | collective-permute-done | bytes 262176 | tf_op jit(solution)/shard_map/ppermute | solution.py:644
  160.7 1.5 collective-permute-done.3.above
  162.3 0.7 copy-done.5
  163.0 0.0 all-to-all-done.7
  163.0 0.0 copy-done
  163.0 0.0 copy-start.1
  163.0 1.2 copy-done.1
  164.2 0.9 copy-done.4
  165.2 0.9 copy-done.6
  166.1 4.4 %air_finish.1 = f32[1024,256]{1,0:T(8,128)} custom-call(s32[2]{0:T(128)S(1)} %pad_add_fusion.place, f32[768,128]{1,0:T(8,128)S(1)} %bitcast.30, f32[1024,256]{1,0:T(8,128)S(1)} %copy-done.1, f32[1024,256]{1,0:T(8,128)S(1)} %bitcast.29, f32[256,256]{1,0:T(8,128)S(1)} %collective-permute-done.2.below, f32[256,256]{1,0:T(8,128)S(1)} %copy-done.6, ...), custom_call_target="tpu_custom_call" | custom-call | tf_op jit(solution)/shard_map/air_finish/pallas_call | solution.py:557
  (10 shorter events, 0.0 us)
Async XLA Ops:
  3.1 19.7 %all-to-all-start = ((f32[128,2,128]{2,1,0:T(2,128)}), f32[128,2,128]{2,1,0:T(2,128)S(1)}, u32[]{:S(2)}, u32[]{:S(2)}) async-start(f32[128,2,128]{2,1,0:T(2,128)} %bitcast.39), calls=%async_computation | async-start | bytes 262144 | tf_op jit(solution)/shard_map/all_to_all | solution.py:581
  24.6 14.1 %all-to-all-start.1 = ((f32[128,2,128]{2,1,0:T(2,128)}), f32[128,2,128]{2,1,0:T(2,128)S(1)}, u32[]{:S(2)}, u32[]{:S(2)}) async-start(f32[128,2,128]{2,1,0:T(2,128)} %bitcast.45), calls=%async_computation.1 | async-start | bytes 262144 | tf_op jit(solution)/shard_map/all_to_all | solution.py:581
  40.3 15.3 %all-to-all-start.2 = ((f32[128,4,128]{2,1,0:T(4,128)}), f32[128,4,128]{2,1,0:T(4,128)S(1)}, u32[]{:S(2)}, u32[]{:S(2)}) async-start(f32[128,4,128]{2,1,0:T(4,128)} %bitcast.43), calls=%async_computation.2 | async-start | bytes 524288 | tf_op jit(solution)/shard_map/all_to_all | solution.py:581
  77.7 14.1 %all-to-all-start.4 = ((f32[128,2,128]{2,1,0:T(2,128)}), f32[128,2,128]{2,1,0:T(2,128)S(1)}, u32[]{:S(2)}, u32[]{:S(2)}) async-start(f32[128,2,128]{2,1,0:T(2,128)} %bitcast.46), calls=%async_computation.4 | async-start | bytes 262144 | tf_op jit(solution)/shard_map/all_to_all | solution.py:581
  93.6 16.6 %all-to-all-start.5 = ((f32[128,3,2,128]{3,2,1,0:T(2,128)}), f32[128,3,2,128]{3,2,1,0:T(2,128)S(1)}, u32[]{:S(2)}, u32[]{:S(2)}) async-start(f32[128,3,2,128]{3,2,1,0:T(2,128)} %bitcast.38), calls=%async_computation.5 | async-start | bytes 786432 | tf_op jit(solution)/shard_map/all_to_all | solution.py:581
  110.2 17.4 %copy-start.2 = (bf16[2,512,512]{2,1,0:T(8,128)(2,1)S(1)}, bf16[2,512,512]{2,1,0:T(8,128)(2,1)}, u32[]{:S(2)}) copy-start(bf16[2,512,512]{2,1,0:T(8,128)(2,1)} %constant.39.clone.refs_3_) | copy-start | bytes 3145732
  129.0 34.0 %all-to-all-start.7 = ((f32[8,96,128]{2,1,0:T(8,128)}), f32[8,96,128]{2,1,0:T(8,128)S(1)}, u32[]{:S(2)}, u32[]{:S(2)}) async-start(f32[8,96,128]{2,1,0:T(8,128)} %bitcast.37), calls=%async_computation.7 | async-start | bytes 786432 | tf_op jit(solution)/shard_map/all_to_all | solution.py:581
  134.4 5.3 %collective-permute-start = (f32[8,256]{1,0:T(8,128)S(1)}, f32[8,256]{1,0:T(8,128)S(1)}, u32[]{:S(2)}, u32[]{:S(2)}) collective-permute-start(f32[8,256]{1,0:T(8,128)S(1)} %get-tuple-element.61), channel_id=1, source_target_pairs={{0,8},{8,16},{16,24},{24,32},{32,40},{40,48},{48,56},{56,64},{64,7... | collective-permute-start | bytes 24584 | tf_op jit(solution)/shard_map/ppermute | solution.py:616
  134.4 5.3 %collective-permute-start.1 = (f32[8,256]{1,0:T(8,128)S(1)}, f32[8,256]{1,0:T(8,128)S(1)}, u32[]{:S(2)}, u32[]{:S(2)}) collective-permute-start(f32[8,256]{1,0:T(8,128)S(1)} %get-tuple-element.60), channel_id=1, source_target_pairs={{8,0},{16,8},{24,16},{32,24},{40,32},{48,40},{56,48},{64,56},{72,6... | collective-permute-start | bytes 24584 | tf_op jit(solution)/shard_map/ppermute | solution.py:617
  139.7 0.6 copy-start.7
  139.7 0.6 copy-start.8
  145.3 17.7 %copy-start = (f32[128,8,256]{2,1,0:T(8,128)S(1)}, f32[128,8,256]{2,1,0:T(8,128)}, u32[]{:S(2)}) copy-start(f32[128,8,256]{2,1,0:T(8,128)} %param.16) | copy-start | bytes 3145732
  145.3 15.5 %collective-permute-start.2 = (f32[256,256]{1,0:T(8,128)}, f32[256,256]{1,0:T(8,128)S(1)}, u32[]{:S(2)}, u32[]{:S(2)}) collective-permute-start(f32[256,256]{1,0:T(8,128)} %get-tuple-element.58.highest_rows), channel_id=1, source_target_pairs={{0,1},{1,2},{2,3},{3,4},{4,5},{5,6},{6,7},{8,9},{9,10},{10,11},{11... | collective-permute-start | bytes 786440 | tf_op jit(solution)/shard_map/ppermute | solution.py:644
  150.3 11.9 %collective-permute-start.3 = (f32[256,256]{1,0:T(8,128)}, f32[256,256]{1,0:T(8,128)S(1)}, u32[]{:S(2)}, u32[]{:S(2)}) collective-permute-start(f32[256,256]{1,0:T(8,128)} %get-tuple-element.59.lowest_rows), channel_id=1, source_target_pairs={{1,0},{2,1},{3,2},{4,3},{5,4},{6,5},{7,6},{9,8},{10,9},{11,10},{12... | collective-permute-start | bytes 786440 | tf_op jit(solution)/shard_map/ppermute | solution.py:645
  153.7 9.2 %copy-start.3 = (f32[256,256]{1,0:T(8,128)S(1)}, f32[256,256]{1,0:T(8,128)}, u32[]{:S(2)}) copy-start(f32[256,256]{1,0:T(8,128)} %get-tuple-element.59.lowest_rows) | copy-start | bytes 786436
  162.2 0.7 copy-start.5
  163.0 1.2 copy-start.1
  164.2 0.9 copy-start.4
  165.2 0.9 copy-start.6
